TPU v7x, 128 devices: a whole 4x4x4 slice. The times are simulated.
128 devices in a mesh: order: 8 (over x_lo, y), chan: 16 (over x_hi, z, core).
Axes of the slice: x: 4 (x_hi: 2, x_lo: 2; x = x_hi * 2 + x_lo), y: 4, z: 4, core: 2. Of those that a mesh axis runs over, the one named last changes fastest.
Arguments:
- grad_out: bfloat16 [3, 256, 720, 1440], P(None, 'chan', 'order'), may hold values from -6 to 6
- legendre: bfloat16 [96, 720, 768], P('order', 'chan'), as said below
- filter_re: float32 [256, 720], P('chan'), may hold values from -6 to 6
- filter_im: float32 [256, 720], P('chan'), may hold values from -6 to 6
- quad_weight: float32 [720], P('order'), may hold values from 0.5 to 2
- pair_order: int32 [96], replicated, may hold values from 0 to 359, as said below
Outputs:
- grad_in: bfloat16 [3, 256, 720, 1440], P(None, 'chan', 'order')
Inputs may be any that keep to these rules, and one draw needn't show every extreme that they name: `pair_order`: the values are distinct. Slot j belongs to index j // 12 of order. `legendre`: entries in rows r > 720 of the last dimension are zero.
All inputs are finite; a program needn't handle non-finite values.
Results may differ from a plain program's by a relative error of at most 0.0072.
Values may be sent and summed in bfloat16 or wider, within the bound.
No kernel may reach another device: no remote copies, remote signals or barrier semaphores. Data moves between devices by JAX's collectives and lax.ppermute only.
A program may use at most 128 MiB of HBM per device.

v0:
```python
import math

import jax
import jax.numpy as jnp
from jax import lax
from jax.experimental import pallas as pl
from jax.experimental.pallas import tpu as pltpu
from jax.sharding import Mesh
from jax.sharding import PartitionSpec as P

NLON = 1440
M = 720
ROWS = 768
PAIRS = 96
SAMPLES = 3
CH = 16
LAT = 90
HALF = 45
HP = 48
DEST = 32
SLOTS = 3
GROUPS = 4
STRIPE = SLOTS * HP
LANES = 128
COLS = 4 * LANES
STEP = 16
CHUNK = 9
VMEM = 56 * 1024 * 1024

SLOT_AXES = ("x_lo", "y", "x_hi", "core")
NT = (((1,), (1,)), ((), ()))
TN = (((0,), (0,)), ((), ()))


def fill_table(low, table, coarse_cos, coarse_sin):
    orders = jnp.concatenate([low, M - 1 - low], axis=1)
    unit = 2.0 * math.pi / NLON

    def angle(count, scale):
        k = lax.broadcasted_iota(jnp.int32, (count, 2 * LANES), 0) * scale
        return lax.rem(k * orders, NLON).astype(jnp.float32) * unit

    coarse = angle(96, STEP)
    coarse_cos[...] = jnp.cos(coarse)
    coarse_sin[...] = jnp.sin(coarse)
    fine = angle(STEP, 1)
    fine_cos, fine_sin = jnp.cos(fine), jnp.sin(fine)

    @pl.loop(0, NLON // STEP)
    def _(a):
        base_cos, base_sin = coarse_cos[pl.ds(a, 1), :], coarse_sin[pl.ds(a, 1), :]
        even = (base_cos * fine_cos - base_sin * fine_sin).astype(table.dtype)
        odd = (-(base_sin * fine_cos) - base_cos * fine_sin).astype(table.dtype)
        rows = pl.ds(pl.multiple_of(a * STEP, STEP), STEP)
        table[rows, :LANES] = even[:, :LANES]
        table[rows, LANES : 2 * LANES] = odd[:, :LANES]
        table[rows, 2 * LANES : 3 * LANES] = even[:, LANES:]
        table[rows, 3 * LANES :] = odd[:, LANES:]


def forward_kernel(low_ref, x_ref, out_ref, table_ref, product, packed, coarse_cos, coarse_sin):
    @pl.when(pl.program_id(0) == 0)
    def _():
        fill_table(low_ref[...], table_ref, coarse_cos, coarse_sin)
        packed[...] = jnp.zeros_like(packed)

    factor = jnp.where(low_ref[...] == 0, 1.0, 2.0).astype(jnp.float32)

    @pl.loop(0, HALF // CHUNK)
    def _(step):
        first = step * CHUNK
        for half in range(2):
            block = x_ref[0, pl.ds(half * HALF + first, CHUNK)].reshape(CHUNK * CH, NLON)
            product[half] = jnp.dot(block, table_ref[...], preferred_element_type=jnp.float32)
        for t in range(CHUNK):
            rows = slice(t * CH, (t + 1) * CH)
            pieces = []
            for q in range(4):
                scale = factor if q < 2 else 2.0
                for half in range(2):
                    pieces.append(product[half, rows, q * LANES : (q + 1) * LANES] * scale)
            turned = jnp.concatenate(pieces, axis=0).T
            for slot in range(SLOTS):
                packed[pl.ds(slot * HP + first + t, DEST, stride=STRIPE), :] = turned[slot * DEST : (slot + 1) * DEST]

    out_ref[...] = packed[...].astype(out_ref.dtype).reshape(out_ref.shape)


def forward(low, grad):
    return pl.pallas_call(
        forward_kernel,
        grid=(SAMPLES,),
        in_specs=[
            pl.BlockSpec((1, LANES), lambda s: (0, 0)),
            pl.BlockSpec((1, LAT, CH, NLON), lambda s: (s, 0, 0, 0)),
        ],
        out_specs=[
            pl.BlockSpec((DEST, 1, STRIPE, LANES), lambda s: (0, s, 0, 0)),
            pl.BlockSpec((NLON, COLS), lambda s: (0, 0)),
        ],
        out_shape=[
            jax.ShapeDtypeStruct((DEST, SAMPLES, STRIPE, LANES), jnp.bfloat16),
            jax.ShapeDtypeStruct((NLON, COLS), jnp.bfloat16),
        ],
        scratch_shapes=[
            pltpu.VMEM((2, CHUNK * CH, COLS), jnp.float32),
            pltpu.VMEM((DEST * STRIPE, LANES), jnp.float32),
            pltpu.VMEM((96, 2 * LANES), jnp.float32),
            pltpu.VMEM((96, 2 * LANES), jnp.float32),
        ],
        compiler_params=pltpu.CompilerParams(vmem_limit_bytes=VMEM),
        cost_estimate=pl.CostEstimate(flops=2 * 4320 * NLON * COLS, bytes_accessed=18_000_000, transcendentals=0),
        name="forward",
    )(low, grad)


def spectral_kernel(low_ref, z_ref, filt_ref, x_ref, t0, t1, t2, t3, out_ref, legendre, columns, gains, sems):
    step = pl.program_id(0)

    def table_copies():
        copies = []
        for k, source in enumerate((t0, t1, t2, t3)):
            z = lax.rem(z_ref[0] + (4 - k), 4)
            for x_hi in range(2):
                for core in range(2):
                    block = x_hi * 8 + z * 2 + core
                    copies.append(
                        pltpu.make_async_copy(source.at[x_hi * 2 + core], legendre.at[:, block], sems.at[k * 4 + x_hi * 2 + core])
                    )
        return copies

    row = lax.broadcasted_iota(jnp.int32, (1, ROWS), 1)

    @pl.when(step == 0)
    def _():
        for copy in table_copies():
            copy.start()
        for slot in range(SLOTS):
            low = low_ref[slot]
            below = row < M - low
            for part in range(2):
                whole = filt_ref[part]
                gains[slot, part] = jnp.where(below, pltpu.roll(whole, ROWS - low, 1), pltpu.roll(whole, 1, 1))
        for copy in table_copies():
            copy.wait()

    lane = lax.broadcasted_iota(jnp.int32, (HP, LANES), 1)
    former_half = lax.rem(lax.div(lane, CH), 2) == 0

    def shuffle(a, b):
        return jnp.where(former_half, a, pltpu.roll(b, CH, 1)), jnp.where(former_half, pltpu.roll(a, LANES - CH, 1), b)

    for slot in range(SLOTS):
        stripe = slice(slot * HP, (slot + 1) * HP)
        for order in range(8):
            for pair in range(2):
                source = order * GROUPS + pair * 2
                a = x_ref[source, 0, stripe, :].astype(jnp.float32)
                b = x_ref[source + 1, 0, stripe, :].astype(jnp.float32)
                lanes = slice(pair * LANES, (pair + 1) * LANES)
                for half, value in enumerate(shuffle(a, b)):
                    block = order * 2 + half
                    columns[block * HP : (block + 1) * HP, lanes] = value.astype(columns.dtype)
        table = legendre[slot].reshape(16 * HP, ROWS)
        spectrum = lax.dot_general(columns[...], table, TN, preferred_element_type=jnp.float32)
        below = row < M - low_ref[slot]
        parts = []
        for pair in range(2):
            a0, a1, a2, a3 = (spectrum[pair * LANES + q * 32 : pair * LANES + (q + 1) * 32] for q in range(4))
            former, latter = jnp.where(below, a0, a2), jnp.where(below, a1, a3)
            re = gains[slot, 0, pair * 32 : (pair + 1) * 32]
            im = gains[slot, 1, pair * 32 : (pair + 1) * 32]
            real, imag = re * former + im * latter, re * latter - im * former
            parts += [jnp.where(below, real, 0.0), jnp.where(below, imag, 0.0)]
            parts += [jnp.where(below, 0.0, real), jnp.where(below, 0.0, imag)]
        split = jnp.concatenate(parts, axis=0).astype(jnp.bfloat16)
        synthesis = lax.dot_general(table, split, NT, preferred_element_type=jnp.float32)
        for order in range(8):
            for pair in range(2):
                lanes = slice(pair * LANES, (pair + 1) * LANES)
                top, mid = order * 2 * HP, (order * 2 + 1) * HP
                target = order * GROUPS + pair * 2
                for offset, value in enumerate(shuffle(synthesis[top:mid, lanes], synthesis[mid : mid + HP, lanes])):
                    out_ref[target + offset, 0, stripe, :] = value.astype(out_ref.dtype)


def spectral(low, z, filters, received, tables):
    shape = (DEST, SAMPLES, STRIPE, LANES)
    block = pl.BlockSpec((DEST, 1, STRIPE, LANES), lambda s: (0, s, 0, 0))
    smem = pl.BlockSpec(memory_space=pltpu.SMEM)
    hbm = pl.BlockSpec(memory_space=pl.ANY)
    return pl.pallas_call(
        spectral_kernel,
        grid=(SAMPLES,),
        in_specs=[smem, smem, pl.BlockSpec((2, GROUPS * CH, ROWS), lambda s: (0, 0, 0)), block, hbm, hbm, hbm, hbm],
        out_specs=block,
        out_shape=jax.ShapeDtypeStruct(shape, jnp.bfloat16),
        scratch_shapes=[
            pltpu.VMEM((SLOTS, 16, HP, ROWS), jnp.bfloat16),
            pltpu.VMEM((16 * HP, 2 * LANES), jnp.bfloat16),
            pltpu.VMEM((SLOTS, 2, GROUPS * CH, ROWS), jnp.float32),
            pltpu.SemaphoreType.DMA((16,)),
        ],
        compiler_params=pltpu.CompilerParams(vmem_limit_bytes=VMEM),
        cost_estimate=pl.CostEstimate(flops=9 * 4 * ROWS * ROWS * 256, bytes_accessed=12_000_000, transcendentals=0),
        name="spectral",
    )(low, z, filters, received, *tables)


def inverse_kernel(scale_ref, table_ref, x_ref, out_ref, packed, left):
    packed[...] = x_ref[...].astype(jnp.float32).reshape(packed.shape)
    blank = jnp.zeros((LANES - PAIRS, LANES), jnp.float32)

    @pl.loop(0, HALF // CHUNK)
    def _(step):
        first = step * CHUNK
        for t in range(CHUNK):
            pieces = [packed[pl.ds(slot * HP + first + t, DEST, stride=STRIPE), :] for slot in range(SLOTS)]
            turned = jnp.concatenate(pieces + [blank], axis=0).T.astype(left.dtype)
            for q in range(4):
                for half in range(2):
                    piece = turned[(q * 2 + half) * CH : (q * 2 + half + 1) * CH]
                    left[half, t * CH : (t + 1) * CH, q * LANES : (q + 1) * LANES] = piece
        for half in range(2):
            values = lax.dot_general(left[half], table_ref[...], NT, preferred_element_type=jnp.float32)
            for t in range(CHUNK):
                lat = half * HALF + first + t
                out_ref[0, lat] = (values[t * CH : (t + 1) * CH] * scale_ref[lat]).astype(out_ref.dtype)


def inverse(scale, table, received):
    return pl.pallas_call(
        inverse_kernel,
        grid=(SAMPLES,),
        in_specs=[
            pl.BlockSpec(memory_space=pltpu.SMEM),
            pl.BlockSpec((NLON, COLS), lambda s: (0, 0)),
            pl.BlockSpec((DEST, 1, STRIPE, LANES), lambda s: (0, s, 0, 0)),
        ],
        out_specs=pl.BlockSpec((1, LAT, CH, NLON), lambda s: (s, 0, 0, 0)),
        out_shape=jax.ShapeDtypeStruct((SAMPLES, LAT, CH, NLON), jnp.bfloat16),
        scratch_shapes=[
            pltpu.VMEM((DEST * STRIPE, LANES), jnp.float32),
            pltpu.VMEM((2, CHUNK * CH, COLS), jnp.bfloat16),
        ],
        compiler_params=pltpu.CompilerParams(vmem_limit_bytes=VMEM),
        cost_estimate=pl.CostEstimate(flops=2 * 4320 * NLON * COLS, bytes_accessed=18_000_000, transcendentals=0),
        name="inverse",
    )(scale, table, received)


def body(grad_out, legendre, filter_re, filter_im, quad_weight, pair_order):
    group = lax.axis_index("x_hi") * 2 + lax.axis_index("core")
    z = lax.axis_index("z")
    mine = (lax.axis_index("x_lo") * 4 + lax.axis_index("y")) * GROUPS + group

    padded = jnp.pad(legendre, ((0, 0), (0, HP - HALF), (0, 0))).reshape(GROUPS, SLOTS, HP, ROWS)
    own = lax.all_to_all(padded, ("x_hi", "core"), 0, 0)
    tables = [own]
    for shift in range(1, 4):
        tables.append(lax.ppermute(own, "z", [(i, (i + shift) % 4) for i in range(4)]))

    filters = jnp.pad(jnp.stack([filter_re, filter_im]), ((0, 0), (0, 0), (0, ROWS - M)))
    filters = lax.all_gather(filters, ("x_hi", "core"), axis=1, tiled=True)

    low_lanes = jnp.pad(pair_order.reshape(DEST, SLOTS).T.reshape(1, PAIRS), ((0, 0), (0, LANES - PAIRS)))
    packed, table = forward(low_lanes, jnp.transpose(grad_out, (0, 2, 1, 3)))
    received = lax.all_to_all(packed, SLOT_AXES, 0, 0)
    low = lax.dynamic_slice_in_dim(pair_order, mine * SLOTS, SLOTS)
    bands = spectral(low, z.reshape(1), filters, received, tables)
    received = lax.all_to_all(bands, SLOT_AXES, 0, 0)
    values = inverse(quad_weight * (2.0 * math.pi / NLON), table, received)
    return jnp.transpose(values, (0, 2, 1, 3))


def solution(mesh):
    fine = Mesh(mesh.devices.reshape(2, 4, 2, 4, 2), ("x_lo", "y", "x_hi", "z", "core"))
    order, chan = ("x_lo", "y"), ("x_hi", "z", "core")
    in_specs = (P(None, chan, order, None), P(order, chan, None), P(chan, None), P(chan, None), P(order), P())
    return jax.shard_map(body, mesh=fine, in_specs=in_specs, out_specs=P(None, chan, order, None), check_vma=False)
```

profile of v0, /device:TPU:1, one launch (start us, length us, event | category | flops | bytes accessed | tf_op | source)
XLA Modules:
  0.0 176.1 jit_solution(16106408514579706673)
XLA Ops:
  0.0 2.2 %pad.14 = bf16[12,48,768]{2,1,0:T(8,128)(2,1)} pad(bf16[12,45,768]{2,1,0:T(8,128)(2,1)} %param.7, bf16[]{:T(256)} %constant.34.clone.1), padding=0_0x0_3x0_0 | pad | bytes 1714178 | tf_op jit(solution)/shard_map/jit(_pad)/pad | solution.py:257
  2.2 5.8 %all-to-all-start.1 = ((bf16[4,3,48,768]{3,2,1,0:T(8,128)(2,1)}), bf16[4,3,48,768]{3,2,1,0:T(8,128)(2,1)S(1)}, u32[]{:S(2)}, u32[]{:S(2)}) async-start(bf16[4,3,48,768]{3,2,1,0:T(8,128)(2,1)} %bitcast.5), calls=%async_computation.1 | async-start | bytes 1769472 | tf_op jit(solution)/shard_map/all_to_all | solution.py:258
  8.0 0.1 reshape.12
  8.1 0.1 copy.8
  8.1 0.1 reshape.13
  8.2 0.6 pad.12.low_ref
  8.8 18.5 %forward.1 = (bf16[32,3,144,128]{3,2,1,0:T(8,128)(2,1)}, bf16[1440,512]{1,0:T(8,128)(2,1)}) custom-call(s32[1,128]{1,0:T(1,128)} %pad.12.low_ref, bf16[3,90,16,1440]{3,2,1,0:T(8,128)(2,1)} %bitcast.10), custom_call_target="tpu_custom_call" | custom-call | flops 6370099200 | bytes 18000000 | tf_op jit(solution)/shard_map/forward/pallas_call | solution.py:90
  27.3 0.0 all-to-all-done.1.t0
  27.3 0.9 copy-done.2
  28.2 7.6 %all-to-all-start = ((bf16[32,3,144,128]{3,2,1,0:T(8,128)(2,1)}), bf16[32,3,144,128]{3,2,1,0:T(8,128)(2,1)S(1)}, u32[]{:S(2)}, u32[]{:S(2)}) async-start(bf16[32,3,144,128]{3,2,1,0:T(8,128)(2,1)} %get-tuple-element.8), calls=%async_computation | async-start | bytes 7077888 | tf_op jit(solution)/shard_map/all_to_all | solution.py:268
  35.8 3.8 %collective-permute-start.2 = (bf16[4,3,48,768]{3,2,1,0:T(8,128)(2,1)}, bf16[4,3,48,768]{3,2,1,0:T(8,128)(2,1)}, u32[]{:S(2)}, u32[]{:S(2)}) collective-permute-start(bf16[4,3,48,768]{3,2,1,0:T(8,128)(2,1)} %copy-done.2), channel_id=1, source_target_pairs={{0,6},{2,0},{4,2},{6,4},{1,7},{3,1},{5,3},{7,5},{8,14},{10,8},{12,... | collective-permute-start | bytes 2654216 | tf_op jit(solution)/shard_map/ppermute | solution.py:261
  39.7 0.7 collective-permute-start
  40.3 0.6 dynamic_slice.3.low_ref
  41.0 0.8 select_maximum_fusion
  41.8 42.9 %all_gather.3.filt_ref = f32[2,64,768]{2,1,0:T(8,128)} all-gather(f32[2,16,768]{2,1,0:T(8,128)S(1)} %select_maximum_fusion), channel_id=1, replica_groups=mesh['x_lo'=2,'y'=4,'x_hi'=2,'z'=4,'core'=2] {'x_hi','core'}, dimensions={1}, use_global_device_ids=true | all-gather | bytes 491520 | tf_op jit(solution)/shard_map/all_gather | solution.py:264
  84.7 0.0 copy-start
  84.7 1.8 %copy-done = bf16[32,3,144,128]{3,2,1,0:T(8,128)(2,1)} copy-done((bf16[32,3,144,128]{3,2,1,0:T(8,128)(2,1)}, bf16[32,3,144,128]{3,2,1,0:T(8,128)(2,1)S(1)}, u32[]{:S(2)}) %copy-start) | copy-done | bytes 3538968
  86.5 13.7 %spectral.1 = bf16[32,3,144,128]{3,2,1,0:T(8,128)(2,1)} custom-call(s32[3]{0:T(128)} %dynamic_slice.3.low_ref, s32[1]{0:T(128)} %bitcast.2.z_ref, f32[2,64,768]{2,1,0:T(8,128)} %all_gather.3.filt_ref, bf16[32,3,144,128]{3,2,1,0:T(8,128)(2,1)} %copy-done, bf16[4,3,48,768]{3,2,1,0:T(8,128)(2,1)} %copy-done.2, bf16[4,3,48,768]{3,2,1,0:T(8,128)(2,1)} %collective-permute-done.t1, ...), custom_call_target="tpu_custom_call" | custom-call | flops 5435817984 | bytes 12000000 | tf_op jit(solution)/shard_map/spectral/pallas_call | solution.py:192
  100.2 0.0 copy-start.4
  100.2 7.0 %all-to-all-start.2 = ((bf16[32,3,144,128]{3,2,1,0:T(8,128)(2,1)}), bf16[32,3,144,128]{3,2,1,0:T(8,128)(2,1)S(1)}, u32[]{:S(2)}, u32[]{:S(2)}) async-start(bf16[32,3,144,128]{3,2,1,0:T(8,128)(2,1)} %spectral.1), calls=%async_computation.2 | async-start | bytes 7077888 | tf_op jit(solution)/shard_map/all_to_all | solution.py:271
  107.2 0.6 broadcast_multiply_fusion.scale_ref
  107.8 45.5 %all-to-all-done.2.x_ref = bf16[32,3,144,128]{3,2,1,0:T(8,128)(2,1)S(1)} async-done(((bf16[32,3,144,128]{3,2,1,0:T(8,128)(2,1)}), bf16[32,3,144,128]{3,2,1,0:T(8,128)(2,1)S(1)}, u32[]{:S(2)}, u32[]{:S(2)}) %all-to-all-start.2) | async-done | bytes 3538976 | tf_op jit(solution)/shard_map/all_to_all | solution.py:271
  153.3 1.7 copy-done.1
  155.0 21.1 %inverse.1 = bf16[3,90,16,1440]{3,2,1,0:T(8,128)(2,1)} custom-call(f32[90]{0:T(128)} %broadcast_multiply_fusion.scale_ref, bf16[1440,512]{1,0:T(8,128)(2,1)} %get-tuple-element.7.table_ref, bf16[32,3,144,128]{3,2,1,0:T(8,128)(2,1)} %copy-done.1), custom_call_target="tpu_custom_call" | custom-call | flops 6370099200 | bytes 18000000 | tf_op jit(solution)/shard_map/inverse/pallas_call | solution.py:232
  (10 shorter events, 0.0 us)
Async XLA Ops:
  0.0 8.0 %copy-start.3 = (s32[96]{0:T(128)S(1)}, s32[96]{0:T(128)}, u32[]{:S(2)}) copy-start(s32[96]{0:T(128)} %param.11) | copy-start | bytes 1156
  2.2 25.1 %all-to-all-start.1 = ((bf16[4,3,48,768]{3,2,1,0:T(8,128)(2,1)}), bf16[4,3,48,768]{3,2,1,0:T(8,128)(2,1)S(1)}, u32[]{:S(2)}, u32[]{:S(2)}) async-start(bf16[4,3,48,768]{3,2,1,0:T(8,128)(2,1)} %bitcast.5), calls=%async_computation.1 | async-start | bytes 1769472 | tf_op jit(solution)/shard_map/all_to_all | solution.py:258
  27.3 0.9 copy-start.2
  28.2 56.4 %all-to-all-start = ((bf16[32,3,144,128]{3,2,1,0:T(8,128)(2,1)}), bf16[32,3,144,128]{3,2,1,0:T(8,128)(2,1)S(1)}, u32[]{:S(2)}, u32[]{:S(2)}) async-start(bf16[32,3,144,128]{3,2,1,0:T(8,128)(2,1)} %get-tuple-element.8), calls=%async_computation | async-start | bytes 7077888 | tf_op jit(solution)/shard_map/all_to_all | solution.py:268
  35.8 48.8 %collective-permute-start.2 = (bf16[4,3,48,768]{3,2,1,0:T(8,128)(2,1)}, bf16[4,3,48,768]{3,2,1,0:T(8,128)(2,1)}, u32[]{:S(2)}, u32[]{:S(2)}) collective-permute-start(bf16[4,3,48,768]{3,2,1,0:T(8,128)(2,1)} %copy-done.2), channel_id=1, source_target_pairs={{0,6},{2,0},{4,2},{6,4},{1,7},{3,1},{5,3},{7,5},{8,14},{10,8},{12,... | collective-permute-start | bytes 2654216 | tf_op jit(solution)/shard_map/ppermute | solution.py:261
  39.7 45.0 %collective-permute-start.1 = (bf16[4,3,48,768]{3,2,1,0:T(8,128)(2,1)}, bf16[4,3,48,768]{3,2,1,0:T(8,128)(2,1)}, u32[]{:S(2)}, u32[]{:S(2)}) collective-permute-start(bf16[4,3,48,768]{3,2,1,0:T(8,128)(2,1)} %copy-done.2), channel_id=1, source_target_pairs={{0,4},{2,6},{4,0},{6,2},{1,5},{3,7},{5,1},{7,3},{8,12},{10,14},{12... | collective-permute-start | bytes 2654216 | tf_op jit(solution)/shard_map/ppermute | solution.py:261
  39.7 45.0 %collective-permute-start = (bf16[4,3,48,768]{3,2,1,0:T(8,128)(2,1)}, bf16[4,3,48,768]{3,2,1,0:T(8,128)(2,1)}, u32[]{:S(2)}, u32[]{:S(2)}) collective-permute-start(bf16[4,3,48,768]{3,2,1,0:T(8,128)(2,1)} %copy-done.2), channel_id=1, source_target_pairs={{0,2},{2,4},{4,6},{6,0},{1,3},{3,5},{5,7},{7,1},{8,10},{10,12},{12... | collective-permute-start | bytes 2654216 | tf_op jit(solution)/shard_map/ppermute | solution.py:261
  84.7 1.8 %copy-start = (bf16[32,3,144,128]{3,2,1,0:T(8,128)(2,1)}, bf16[32,3,144,128]{3,2,1,0:T(8,128)(2,1)S(1)}, u32[]{:S(2)}) copy-start(bf16[32,3,144,128]{3,2,1,0:T(8,128)(2,1)S(1)} %all-to-all-done.x_ref) | copy-start | bytes 10616836
  100.2 7.0 %copy-start.4 = (f32[90]{0:T(128)S(1)}, f32[90]{0:T(128)}, u32[]{:S(2)}) copy-start(f32[90]{0:T(128)} %param.10) | copy-start | bytes 1084
  100.2 53.1 %all-to-all-start.2 = ((bf16[32,3,144,128]{3,2,1,0:T(8,128)(2,1)}), bf16[32,3,144,128]{3,2,1,0:T(8,128)(2,1)S(1)}, u32[]{:S(2)}, u32[]{:S(2)}) async-start(bf16[32,3,144,128]{3,2,1,0:T(8,128)(2,1)} %spectral.1), calls=%async_computation.2 | async-start | bytes 7077888 | tf_op jit(solution)/shard_map/all_to_all | solution.py:271
  153.3 1.7 copy-start.1
where the time goes:
time: 177 us; the launch traced here: 176 us
  Pallas kernels  53.3 us (30%)
  waiting for transfers between devices  45.5 us (26%)
  blocking collectives  42.9 us (24%)
  starting transfers between devices  24.9 us (14%)
  local copies, waits for them, and re-layouts  8.11 us (5%)
    all_to_all x1, waiting for transfers between devices, body(): received = lax.all_to_all(bands, SLOT_AXES, 0, 0)  45.5 us
    all_gather x1, blocking collectives, body(): filters = lax.all_gather(filters, ('x_hi', 'core'), axis=1, tiled=True)  42.9 us
    pallas_call x1, Pallas kernels, inverse(): pl.pallas_call(inverse_kernel, grid=(SAMPLES,), in_specs=[pl.BlockSpec(me...  21.1 us
    pallas_call x1, Pallas kernels, forward(): pl.pallas_call(forward_kernel, grid=(SAMPLES,), in_specs=[pl.BlockSpec((1...  18.5 us
    pallas_call x1, Pallas kernels, spectral(): pl.pallas_call(spectral_kernel, grid=(SAMPLES,), in_specs=[smem, smem, pl...  13.7 us
    all_to_all x1, starting transfers between devices, body(): received = lax.all_to_all(packed, SLOT_AXES, 0, 0)  7.59 us
    all_to_all x1, starting transfers between devices, body(): received = lax.all_to_all(bands, SLOT_AXES, 0, 0)  7.02 us
    all_to_all x1, starting transfers between devices, body(): own = lax.all_to_all(padded, ('x_hi', 'core'), 0, 0)  5.79 us
  transfers between devices with their start and end apart: 6, of which 1 were waited for; matrix products, arithmetic and copies ran while one was open for 2% of the time, Pallas kernels for 10%

commit v1 on v0

v1 whole, which is shorter than its diff:
```python
import math

import jax
import jax.numpy as jnp
from jax import lax
from jax.experimental import pallas as pl
from jax.experimental.pallas import tpu as pltpu
from jax.sharding import Mesh
from jax.sharding import PartitionSpec as P

NLON = 1440
M = 720
ROWS = 768
PAIRS = 96
SAMPLES = 3
EARLY = 2
CH = 16
LAT = 90
HALF = 45
HP = 48
DEST = 32
SLOTS = 3
GROUPS = 4
STRIPE = SLOTS * HP
LANES = 128
COLS = 4 * LANES
STEP = 16
CHUNK = 9
VMEM = 63 * 1024 * 1024

SLOT_AXES = ("x_lo", "y", "x_hi", "core")
NT = (((1,), (1,)), ((), ()))
TN = (((0,), (0,)), ((), ()))


def fill_table(low, table, coarse_cos, coarse_sin):
    orders = jnp.concatenate([low, M - 1 - low], axis=1)
    unit = 2.0 * math.pi / NLON

    def angle(count, scale):
        k = lax.broadcasted_iota(jnp.int32, (count, 2 * LANES), 0) * scale
        return lax.rem(k * orders, NLON).astype(jnp.float32) * unit

    coarse = angle(96, STEP)
    coarse_cos[...] = jnp.cos(coarse)
    coarse_sin[...] = jnp.sin(coarse)
    fine = angle(STEP, 1)
    fine_cos, fine_sin = jnp.cos(fine), jnp.sin(fine)

    @pl.loop(0, NLON // STEP)
    def _(a):
        base_cos, base_sin = coarse_cos[pl.ds(a, 1), :], coarse_sin[pl.ds(a, 1), :]
        even = (base_cos * fine_cos - base_sin * fine_sin).astype(table.dtype)
        odd = (-(base_sin * fine_cos) - base_cos * fine_sin).astype(table.dtype)
        rows = pl.ds(pl.multiple_of(a * STEP, STEP), STEP)
        table[rows, :LANES] = even[:, :LANES]
        table[rows, LANES : 2 * LANES] = odd[:, :LANES]
        table[rows, 2 * LANES : 3 * LANES] = even[:, LANES:]
        table[rows, 3 * LANES :] = odd[:, LANES:]


def first_forward_kernel(low_ref, x_ref, out_ref, table_ref, product, packed, coarse_cos, coarse_sin):
    @pl.when(pl.program_id(0) == 0)
    def _():
        fill_table(low_ref[...], table_ref, coarse_cos, coarse_sin)
        packed[...] = jnp.zeros_like(packed)

    transform(low_ref, x_ref, table_ref, out_ref, product, packed)


def later_forward_kernel(low_ref, x_ref, table_ref, out_ref, product, packed):
    @pl.when(pl.program_id(0) == 0)
    def _():
        packed[...] = jnp.zeros_like(packed)

    transform(low_ref, x_ref, table_ref, out_ref, product, packed)


def transform(low_ref, x_ref, table_ref, out_ref, product, packed):
    factor = jnp.where(low_ref[...] == 0, 1.0, 2.0).astype(jnp.float32)

    @pl.loop(0, 2)
    def _(half):
        block = x_ref[0, pl.ds(half * HALF, HALF)].reshape(HALF * CH, NLON)
        rows = pl.ds(pl.multiple_of(half * HALF * CH, CH), HALF * CH)
        product[rows, :] = jnp.dot(block, table_ref[...], preferred_element_type=jnp.float32)

    @pl.loop(0, HALF // CHUNK)
    def _(step):
        first = step * CHUNK
        for t in range(CHUNK):
            pieces = []
            for q in range(4):
                scale = factor if q < 2 else 2.0
                for half in range(2):
                    rows = pl.ds(pl.multiple_of((half * HALF + first + t) * CH, CH), CH)
                    pieces.append(product[rows, q * LANES : (q + 1) * LANES] * scale)
            turned = jnp.concatenate(pieces, axis=0).T
            for slot in range(SLOTS):
                packed[pl.ds(slot * HP + first + t, DEST, stride=STRIPE), :] = turned[slot * DEST : (slot + 1) * DEST]

    out_ref[...] = packed[...].astype(out_ref.dtype).reshape(out_ref.shape)


def forward(low, grad, start, count, table=None):
    whole = pl.BlockSpec((NLON, COLS), lambda s: (0, 0))
    in_specs = [pl.BlockSpec((1, LANES), lambda s: (0, 0)), pl.BlockSpec((1, LAT, CH, NLON), lambda s: (s + start, 0, 0, 0))]
    out_specs = [pl.BlockSpec((DEST, 1, STRIPE, LANES), lambda s: (0, s, 0, 0))]
    out_shape = [jax.ShapeDtypeStruct((DEST, count, STRIPE, LANES), jnp.bfloat16)]
    scratch = [pltpu.VMEM((LAT * CH, COLS), jnp.float32), pltpu.VMEM((DEST * STRIPE, LANES), jnp.float32)]
    if table is None:
        out_specs.append(whole)
        out_shape.append(jax.ShapeDtypeStruct((NLON, COLS), jnp.bfloat16))
        scratch += [pltpu.VMEM((96, 2 * LANES), jnp.float32)] * 2
    else:
        in_specs.append(whole)
    return pl.pallas_call(
        first_forward_kernel if table is None else later_forward_kernel,
        grid=(count,),
        in_specs=in_specs,
        out_specs=out_specs,
        out_shape=out_shape,
        scratch_shapes=scratch,
        compiler_params=pltpu.CompilerParams(vmem_limit_bytes=VMEM),
        cost_estimate=pl.CostEstimate(flops=4 * count * 1440 * NLON * COLS, bytes_accessed=count * 6_000_000, transcendentals=0),
        name="forward",
    )(low, grad, *([] if table is None else [table]))


def spectral_kernel(low_ref, place_ref, f0, f1, x_ref, t0, t1, t2, t3, out_ref, legendre, columns, split, synthesis, gains, sems):
    slot = pl.program_id(0)
    group, z = place_ref[0], place_ref[1]

    def table_copies(which):
        copies = []
        for k in range(GROUPS):
            other = jnp.bitwise_xor(group, k)
            for shift, source in enumerate((t0, t1, t2, t3)):
                block = lax.div(other, 2) * 8 + lax.rem(z + (4 - shift), 4) * 2 + lax.rem(other, 2)
                copies.append(pltpu.make_async_copy(source.at[k, which], legendre.at[which, block], sems.at[which, k * 4 + shift]))
        return copies

    @pl.when(slot == 0)
    def _():
        for which in range(SLOTS):
            for copy in table_copies(which):
                copy.start()

    low = low_ref[slot]
    below = lax.broadcasted_iota(jnp.int32, (1, ROWS), 1) < M - low
    for k in range(GROUPS):
        rows = pl.ds(pl.multiple_of(jnp.bitwise_xor(group, k) * CH, CH), CH)
        for part in range(2):
            whole = (f1 if k % 2 else f0)[k // 2, part]
            gains[part, rows, :] = jnp.where(below, pltpu.roll(whole, ROWS - low, 1), pltpu.roll(whole, 1, 1))

    lane = lax.broadcasted_iota(jnp.int32, (HP, LANES), 1)
    former_half = lax.rem(lax.div(lane, CH), 2) == 0

    def shuffle(a, b):
        return jnp.where(former_half, a, pltpu.roll(b, CH, 1)), jnp.where(former_half, pltpu.roll(a, LANES - CH, 1), b)

    samples = x_ref.shape[1]
    tiles = [(sample, pair, slice((sample * 2 + pair) * LANES, (sample * 2 + pair + 1) * LANES)) for sample in range(samples) for pair in range(2)]

    @pl.loop(0, 8)
    def _(order):
        for sample, pair, lanes in tiles:
            a = x_ref[order * GROUPS + pair * 2, sample].astype(jnp.float32)
            b = x_ref[order * GROUPS + pair * 2 + 1, sample].astype(jnp.float32)
            for half, value in enumerate(shuffle(a, b)):
                rows = pl.ds(pl.multiple_of((order * 2 + half) * HP, HP), HP)
                columns[rows, lanes] = value.astype(columns.dtype)

    for copy in table_copies(slot):
        copy.wait()
    table = legendre[slot].reshape(16 * HP, ROWS)
    spectrum = lax.dot_general(columns[...], table, TN, preferred_element_type=jnp.float32)
    for sample, pair, lanes in tiles:
        a0, a1, a2, a3 = (spectrum[lanes.start + q * 32 : lanes.start + (q + 1) * 32] for q in range(4))
        former, latter = jnp.where(below, a0, a2), jnp.where(below, a1, a3)
        re = gains[0, pair * 32 : (pair + 1) * 32]
        im = gains[1, pair * 32 : (pair + 1) * 32]
        real, imag = re * former + im * latter, re * latter - im * former
        parts = (jnp.where(below, real, 0.0), jnp.where(below, imag, 0.0), jnp.where(below, 0.0, real), jnp.where(below, 0.0, imag))
        for q in range(4):
            split[lanes.start + q * 32 : lanes.start + (q + 1) * 32, :] = parts[q].astype(split.dtype)
    synthesis[...] = lax.dot_general(table, split[...], NT, preferred_element_type=jnp.float32)

    @pl.loop(0, 8)
    def _(order):
        for sample, pair, lanes in tiles:
            halves = [synthesis[pl.ds(pl.multiple_of((order * 2 + half) * HP, HP), HP), lanes] for half in range(2)]
            for offset, value in enumerate(shuffle(*halves)):
                out_ref[order * GROUPS + pair * 2 + offset, sample] = value.astype(out_ref.dtype)


def spectral(low, place, filters, received, tables):
    count = received.shape[1]
    width = count * 2 * LANES
    block = pl.BlockSpec((DEST, count, HP, LANES), lambda slot: (0, 0, slot, 0))
    smem = pl.BlockSpec(memory_space=pltpu.SMEM)
    hbm = pl.BlockSpec(memory_space=pl.ANY)
    gain = pl.BlockSpec((2, 2, CH, ROWS), lambda slot: (0, 0, 0, 0))
    return pl.pallas_call(
        spectral_kernel,
        grid=(SLOTS,),
        in_specs=[smem, smem] + [gain] * 2 + [block] + [hbm] * 4,
        out_specs=block,
        out_shape=jax.ShapeDtypeStruct(received.shape, jnp.bfloat16),
        scratch_shapes=[
            pltpu.VMEM((SLOTS, 16, HP, ROWS), jnp.bfloat16),
            pltpu.VMEM((16 * HP, width), jnp.bfloat16),
            pltpu.VMEM((width, ROWS), jnp.bfloat16),
            pltpu.VMEM((16 * HP, width), jnp.float32),
            pltpu.VMEM((2, GROUPS * CH, ROWS), jnp.float32),
            pltpu.SemaphoreType.DMA((SLOTS, 16)),
        ],
        compiler_params=pltpu.CompilerParams(vmem_limit_bytes=VMEM),
        cost_estimate=pl.CostEstimate(flops=12 * ROWS * ROWS * width, bytes_accessed=12_000_000, transcendentals=0),
        name="spectral",
    )(low, place, *filters, received, *tables)


def later_inverse_kernel(scale_ref, table_ref, x_ref, done_ref, out_ref, packed, left):
    inverse_kernel(scale_ref, table_ref, x_ref, out_ref, packed, left)


def inverse_kernel(scale_ref, table_ref, x_ref, out_ref, packed, left):
    packed[...] = x_ref[...].astype(jnp.float32).reshape(packed.shape)
    blank = jnp.zeros((LANES - PAIRS, LANES), jnp.float32)

    @pl.loop(0, HALF // CHUNK)
    def _(step):
        first = step * CHUNK
        for t in range(CHUNK):
            pieces = [packed[pl.ds(slot * HP + first + t, DEST, stride=STRIPE), :] for slot in range(SLOTS)]
            turned = jnp.concatenate(pieces + [blank], axis=0).T.astype(left.dtype)
            for q in range(4):
                for half in range(2):
                    piece = turned[(q * 2 + half) * CH : (q * 2 + half + 1) * CH]
                    rows = pl.ds(pl.multiple_of((half * HALF + first + t) * CH, CH), CH)
                    left[rows, q * LANES : (q + 1) * LANES] = piece

    @pl.loop(0, 2)
    def _(half):
        rows = pl.ds(pl.multiple_of(half * HALF * CH, CH), HALF * CH)
        scale = scale_ref[pl.ds(half * HALF, HALF)]
        for start in range(0, NLON, 512):
            stop = min(start + 512, NLON)
            values = lax.dot_general(left[rows, :], table_ref[start:stop, :], NT, preferred_element_type=jnp.float32)
            values = values.reshape(HALF, CH, stop - start) * scale[:, :, : stop - start]
            out_ref[0, pl.ds(half * HALF, HALF), :, start:stop] = values.astype(out_ref.dtype)


def inverse(scale, table, received, start, done=None):
    count = received.shape[1]
    in_specs = [
        pl.BlockSpec((LAT, 1, 512), lambda s: (0, 0, 0)),
        pl.BlockSpec((NLON, COLS), lambda s: (0, 0)),
        pl.BlockSpec((DEST, 1, STRIPE, LANES), lambda s: (0, s, 0, 0)),
    ]
    return pl.pallas_call(
        inverse_kernel if done is None else later_inverse_kernel,
        grid=(count,),
        in_specs=in_specs if done is None else in_specs + [pl.BlockSpec(memory_space=pl.ANY)],
        out_specs=pl.BlockSpec((1, LAT, CH, NLON), lambda s: (s + start, 0, 0, 0)),
        out_shape=jax.ShapeDtypeStruct((SAMPLES, LAT, CH, NLON), jnp.bfloat16),
        input_output_aliases={} if done is None else {3: 0},
        scratch_shapes=[
            pltpu.VMEM((DEST * STRIPE, LANES), jnp.float32),
            pltpu.VMEM((LAT * CH, COLS), jnp.bfloat16),
        ],
        compiler_params=pltpu.CompilerParams(vmem_limit_bytes=VMEM),
        cost_estimate=pl.CostEstimate(flops=4 * count * 1440 * NLON * COLS, bytes_accessed=count * 6_000_000, transcendentals=0),
        name="inverse",
    )(scale, table, received, *([] if done is None else [done]))


def body(grad_out, legendre, filter_re, filter_im, quad_weight, pair_order):
    group = lax.axis_index("x_hi") * 2 + lax.axis_index("core")
    z = lax.axis_index("z")
    mine = (lax.axis_index("x_lo") * 4 + lax.axis_index("y")) * GROUPS + group

    by_group = legendre.reshape(GROUPS, SLOTS, HALF, ROWS)
    pieces = []
    for k in range(GROUPS):
        piece = lax.dynamic_index_in_dim(by_group, jnp.bitwise_xor(group, k), 0, keepdims=False)
        pieces.append(lax.ppermute(piece, ("x_hi", "core"), [(i, i ^ k) for i in range(GROUPS)]) if k else piece)
    filters = jnp.pad(jnp.stack([filter_re, filter_im]), ((0, 0), (0, 0), (0, ROWS - M)))
    filters = [filters, lax.ppermute(filters, "x_hi", [(0, 1), (1, 0)])]

    low_lanes = jnp.pad(pair_order.reshape(DEST, SLOTS).T.reshape(1, PAIRS), ((0, 0), (0, LANES - PAIRS)))
    grad = jnp.transpose(grad_out, (0, 2, 1, 3))
    packed, table = forward(low_lanes, grad, 0, EARLY)
    packed, pieces, filters = lax.optimization_barrier((packed, pieces, filters))
    early = lax.all_to_all(packed, SLOT_AXES, 0, 0)
    own = jnp.pad(jnp.stack(pieces), ((0, 0), (0, 0), (0, HP - HALF), (0, 0)))
    near = jnp.stack(filters)
    tables = [own] + [lax.ppermute(own, "z", [(i, (i + shift) % 4) for i in range(4)]) for shift in range(1, 4)]
    (packed,) = forward(low_lanes, grad, EARLY, SAMPLES - EARLY, table)
    filters = [near, lax.ppermute(near, "core", [(0, 1), (1, 0)])]
    late = lax.all_to_all(packed, SLOT_AXES, 0, 0)

    low = lax.dynamic_slice_in_dim(pair_order, mine * SLOTS, SLOTS)
    place = jnp.stack([group, z])
    early = lax.all_to_all(spectral(low, place, filters, early, tables), SLOT_AXES, 0, 0)
    late = lax.all_to_all(spectral(low, place, filters, late, tables), SLOT_AXES, 0, 0)

    scale = jnp.broadcast_to((quad_weight * (2.0 * math.pi / NLON))[:, None, None], (LAT, 1, 512))
    values = inverse(scale, table, early, 0)
    values = inverse(scale, table, late, EARLY, values)
    return jnp.transpose(values, (0, 2, 1, 3))


def solution(mesh):
    fine = Mesh(mesh.devices.reshape(2, 4, 2, 4, 2), ("x_lo", "y", "x_hi", "z", "core"))
    order, chan = ("x_lo", "y"), ("x_hi", "z", "core")
    in_specs = (P(None, chan, order, None), P(order, chan, None), P(chan, None), P(chan, None), P(order), P())
    return jax.shard_map(body, mesh=fine, in_specs=in_specs, out_specs=P(None, chan, order, None), check_vma=False)
```

time: 177 us -> 163 us (0.921)
  blocking collectives: 42.9 us -> 0 us
  starting transfers between devices: 24.9 us -> 37.7 us
  Pallas kernels: 53.3 us -> 64.1 us
  waiting for transfers between devices: 45.5 us -> 51.7 us
  local copies, waits for them, and re-layouts: 8.11 us -> 5.17 us
  other arithmetic: 1.41 us -> 3.56 us
    all_gather x1 -> x0, blocking collectives: 42.9 us -> none  [body(): filters = lax.all_gather(filters, ('x_hi', 'core'), axis=1, tiled=True)]
    pallas_call x3 -> x6, Pallas kernels: 53.3 us -> 64.1 us  [the longest x2 23.6 us: spectral(): pl.pallas_call(spectral_kernel, grid=(SLOTS,), in_specs=[smem, smem] + [g...]
    ppermute x0 -> x5, starting transfers between devices: none -> 7.85 us  [the longest x3 3.81 us: body(): lax.ppermute(piece, ('x_hi', 'core'), [(i, i ^ k) for i in range(GROUPS)])]
    ppermute x3, waiting for transfers between devices: 0.01 us -> 6.55 us  [body(): lax.ppermute(own, 'z', [(i, (i + shift) % 4) for i in range(4)])]
    all_to_all x3 -> x4, starting transfers between devices: 20.4 us -> 25.3 us  [the longest x1 7.85 us: body(): lax.all_to_all(spectral(low, place, filters, early, tables), SLOT_AXES, 0...]
    unnamed x10 -> x20, local copies, waits for them, and re-layouts: 4.49 us -> 0.83 us
    another operation x0 -> x3, other arithmetic: none -> 2.71 us  [the longest x1 1.23 us: body(): own = jnp.pad(jnp.stack(pieces), ((0, 0), (0, 0), (0, HP - HALF), (0, 0)))]
    pad x1 -> x0, local copies, waits for them, and re-layouts: 2.15 us -> none  [body(): jnp.pad(legendre, ((0, 0), (0, HP - HALF), (0, 0)))]
  transfers between devices with their start and end apart: 6 -> 12, of which waited for: 1 -> 5; matrix products, arithmetic and copies ran while one was open for 2% -> 4% of each run, Pallas kernels for 10% -> 35%
where the time goes in v1:
time: 163 us; the launch traced here: 162 us
  Pallas kernels  64.1 us (39%)
  waiting for transfers between devices  51.7 us (32%)
  starting transfers between devices  37.7 us (23%)
  local copies, waits for them, and re-layouts  5.17 us (3%)
  other arithmetic  3.56 us (2%)
    pallas_call x2, Pallas kernels, spectral(): pl.pallas_call(spectral_kernel, grid=(SLOTS,), in_specs=[smem, smem] + [g...  23.6 us
    all_to_all x1, waiting for transfers between devices, body(): lax.all_to_all(spectral(low, place, filters, early, tables), SLOT_AXES, 0...  21.1 us
    pallas_call x2, Pallas kernels, forward(): pl.pallas_call(first_forward_kernel if table is None else later_forward_k...  21.1 us
    pallas_call x2, Pallas kernels, inverse(): pl.pallas_call(inverse_kernel if done is None else later_inverse_kernel,...  19.4 us
    all_to_all x1, waiting for transfers between devices, body(): early = lax.all_to_all(packed, SLOT_AXES, 0, 0)  18.1 us
    all_to_all x1, starting transfers between devices, body(): lax.all_to_all(spectral(low, place, filters, early, tables), SLOT_AXES, 0...  7.85 us
    ppermute x3, waiting for transfers between devices, body(): lax.ppermute(own, 'z', [(i, (i + shift) % 4) for i in range(4)])  6.55 us
    all_to_all x1, waiting for transfers between devices, body(): lax.all_to_all(spectral(low, place, filters, late, tables), SLOT_AXES, 0, 0)  5.97 us
  transfers between devices with their start and end apart: 12, of which 5 were waited for; matrix products, arithmetic and copies ran while one was open for 4% of the time, Pallas kernels for 35%

profile of v1, /device:TPU:1, one launch (start us, length us, event | category | flops | bytes accessed | tf_op | source)
XLA Modules:
  0.0 162.4 jit_solution(1259553987802401133)
XLA Ops:
  0.0 0.8 select_maximum_fusion
  0.8 3.7 %collective-permute-start.3 = (f32[2,16,768]{2,1,0:T(8,128)S(1)}, f32[2,16,768]{2,1,0:T(8,128)}, u32[]{:S(2)}, u32[]{:S(2)}) collective-permute-start(f32[2,16,768]{2,1,0:T(8,128)S(1)} %select_maximum_fusion), channel_id=1, source_target_pairs={{0,8},{8,0},{1,9},{9,1},{2,10},{10,2},{3,11},{11,3},{4,12},{12,4},... | collective-permute-start | bytes 294920 | tf_op jit(solution)/shard_map/ppermute | solution.py:291
  4.5 2.1 %dynamic-slice_bitcast_fusion = (bf16[3,45,768]{2,1,0:T(8,128)(2,1)}, bf16[3,45,768]{2,1,0:T(8,128)(2,1)}, bf16[3,45,768]{2,1,0:T(8,128)(2,1)S(1)}, bf16[3,45,768]{2,1,0:T(8,128)(2,1)}) fusion(bf16[4,3,45,768]{3,2,1,0:T(8,128)(2,1)} %bitcast.24, s32[]{:T(128)S(6)} %select_n.20, s32[]{:T(128)S(6)} %select_n.19, s32[]{:T(128)S(6)} %select_n.18, s32[]{:T(128)S(6)} %select_n.17), kind=kLoop, calls=%fused_computation.8 | loop fusion | bytes 1658896 | tf_op jit(solution)/shard_map/jit(dynamic_index_in_dim)/squeeze | solution.py:288
  6.6 1.0 collective-permute-start.2
  7.6 2.8 %collective-permute-start.1 = (bf16[3,45,768]{2,1,0:T(8,128)(2,1)}, bf16[3,45,768]{2,1,0:T(8,128)(2,1)S(1)}, u32[]{:S(2)}, u32[]{:S(2)}) collective-permute-start(bf16[3,45,768]{2,1,0:T(8,128)(2,1)} %get-tuple-element.24), channel_id=1, source_target_pairs={{0,8},{1,9},{8,0},{9,1},{2,10},{3,11},{10,2},{11,3},{4,12},{5,13},... | collective-permute-start | bytes 622088 | tf_op jit(solution)/shard_map/ppermute | solution.py:289
  11.2 13.2 %forward.2 = (bf16[32,2,144,128]{3,2,1,0:T(8,128)(2,1)}, bf16[1440,512]{1,0:T(8,128)(2,1)}) custom-call(s32[1,128]{1,0:T(1,128)} %pad.12.low_ref, bf16[3,90,16,1440]{3,2,1,0:T(8,128)(2,1)} %bitcast.22), custom_call_target="tpu_custom_call" | custom-call | flops 8493465600 | bytes 12000000 | tf_op jit(solution)/shard_map/forward/pallas_call | solution.py:117
  25.3 5.8 %all-to-all-start.2 = ((bf16[32,2,144,128]{3,2,1,0:T(8,128)(2,1)}), bf16[32,2,144,128]{3,2,1,0:T(8,128)(2,1)}, u32[]{:S(2)}, u32[]{:S(2)}) async-start(bf16[32,2,144,128]{3,2,1,0:T(8,128)(2,1)} %get-tuple-element.22), calls=%async_computation.2 | async-start | bytes 4718592 | tf_op jit(solution)/shard_map/all_to_all | solution.py:297
  31.1 1.2 fusion.6.t0
  32.3 3.8 %collective-permute-start.7 = (bf16[4,3,48,768]{3,2,1,0:T(8,128)(2,1)S(1)}, bf16[4,3,48,768]{3,2,1,0:T(8,128)(2,1)}, u32[]{:S(2)}, u32[]{:S(2)}) collective-permute-start(bf16[4,3,48,768]{3,2,1,0:T(8,128)(2,1)S(1)} %fusion.6.t0), channel_id=1, source_target_pairs={{0,6},{2,0},{4,2},{6,4},{1,7},{3,1},{5,3},{7,5},{8,14},{10,8},{12,... | collective-permute-start | bytes 2654216 | tf_op jit(solution)/shard_map/ppermute | solution.py:300
  36.8 7.9 %forward.3 = bf16[32,1,144,128]{3,2,1,0:T(8,128)(2,1)} custom-call(s32[1,128]{1,0:T(1,128)} %pad.12.low_ref, bf16[3,90,16,1440]{3,2,1,0:T(8,128)(2,1)} %bitcast.23, bf16[1440,512]{1,0:T(8,128)(2,1)} %get-tuple-element.14.table_ref), custom_call_target="tpu_custom_call" | custom-call | flops 4246732800 | bytes 6000000 | tf_op jit(solution)/shard_map/forward/pallas_call | solution.py:117
  44.7 18.1 %all-to-all-done.2.x_ref = bf16[32,2,144,128]{3,2,1,0:T(8,128)(2,1)} async-done(((bf16[32,2,144,128]{3,2,1,0:T(8,128)(2,1)}), bf16[32,2,144,128]{3,2,1,0:T(8,128)(2,1)}, u32[]{:S(2)}, u32[]{:S(2)}) %all-to-all-start.2) | async-done | bytes 2359328 | tf_op jit(solution)/shard_map/all_to_all | solution.py:297
  62.8 5.8 %all-to-all-start = ((bf16[32,1,144,128]{3,2,1,0:T(8,128)(2,1)}), bf16[32,1,144,128]{3,2,1,0:T(8,128)(2,1)}, u32[]{:S(2)}, u32[]{:S(2)}) async-start(bf16[32,1,144,128]{3,2,1,0:T(8,128)(2,1)} %forward.3), calls=%async_computation | async-start | bytes 2359296 | tf_op jit(solution)/shard_map/all_to_all | solution.py:303
  68.7 0.9 pad_maximum_fusion.f0
  71.1 2.7 %collective-permute-done.7.t3 = bf16[4,3,48,768]{3,2,1,0:T(8,128)(2,1)} collective-permute-done((bf16[4,3,48,768]{3,2,1,0:T(8,128)(2,1)S(1)}, bf16[4,3,48,768]{3,2,1,0:T(8,128)(2,1)}, u32[]{:S(2)}, u32[]{:S(2)}) %collective-permute-start.7) | collective-permute-done | bytes 884768 | tf_op jit(solution)/shard_map/ppermute | solution.py:300
  73.9 3.8 %collective-permute-done.5.t1 = bf16[4,3,48,768]{3,2,1,0:T(8,128)(2,1)} collective-permute-done((bf16[4,3,48,768]{3,2,1,0:T(8,128)(2,1)S(1)}, bf16[4,3,48,768]{3,2,1,0:T(8,128)(2,1)}, u32[]{:S(2)}, u32[]{:S(2)}) %collective-permute-start.5) | collective-permute-done | bytes 884768 | tf_op jit(solution)/shard_map/ppermute | solution.py:300
  77.7 13.0 %spectral.3 = bf16[32,2,144,128]{3,2,1,0:T(8,128)(2,1)} custom-call(s32[3]{0:T(128)} %dynamic_slice.16.low_ref, s32[2]{0:T(128)} %pad_add_fusion.place_ref, f32[2,2,16,768]{3,2,1,0:T(8,128)} %copy-done.5, f32[2,2,16,768]{3,2,1,0:T(8,128)} %copy-done.8, bf16[32,2,144,128]{3,2,1,0:T(8,128)(2,1)} %all-to-all-done.2.x_ref, bf16[4,3,48,768]{3,2,1,0:T(8,128)(2,1)} %copy-done, ...), custom_call_target="tpu_custom_call" | custom-call | flops 3623878656 | bytes 12000000 | tf_op jit(solution)/shard_map/spectral/pallas_call | solution.py:205
  90.7 7.9 %all-to-all-start.3 = ((bf16[32,2,144,128]{3,2,1,0:T(8,128)(2,1)}), bf16[32,2,144,128]{3,2,1,0:T(8,128)(2,1)}, u32[]{:S(2)}, u32[]{:S(2)}) async-start(bf16[32,2,144,128]{3,2,1,0:T(8,128)(2,1)} %spectral.3), calls=%async_computation.3 | async-start | bytes 4718592 | tf_op jit(solution)/shard_map/all_to_all | solution.py:307
  98.5 10.6 %spectral.2 = bf16[32,1,144,128]{3,2,1,0:T(8,128)(2,1)} custom-call(s32[3]{0:T(128)} %dynamic_slice.16.low_ref, s32[2]{0:T(128)} %pad_add_fusion.place_ref, f32[2,2,16,768]{3,2,1,0:T(8,128)} %copy-done.5, f32[2,2,16,768]{3,2,1,0:T(8,128)} %copy-done.8, bf16[32,1,144,128]{3,2,1,0:T(8,128)(2,1)} %all-to-all-done.x_ref, bf16[4,3,48,768]{3,2,1,0:T(8,128)(2,1)} %copy-done, ...), custom_call_target="tpu_custom_call" | custom-call | flops 1811939328 | bytes 12000000 | tf_op jit(solution)/shard_map/spectral/pallas_call | solution.py:205
  109.2 21.1 %all-to-all-done.3.x_ref = bf16[32,2,144,128]{3,2,1,0:T(8,128)(2,1)} async-done(((bf16[32,2,144,128]{3,2,1,0:T(8,128)(2,1)}), bf16[32,2,144,128]{3,2,1,0:T(8,128)(2,1)}, u32[]{:S(2)}, u32[]{:S(2)}) %all-to-all-start.3) | async-done | bytes 2359328 | tf_op jit(solution)/shard_map/all_to_all | solution.py:307
  130.3 5.8 %all-to-all-start.1 = ((bf16[32,1,144,128]{3,2,1,0:T(8,128)(2,1)}), bf16[32,1,144,128]{3,2,1,0:T(8,128)(2,1)}, u32[]{:S(2)}, u32[]{:S(2)}) async-start(bf16[32,1,144,128]{3,2,1,0:T(8,128)(2,1)} %spectral.2), calls=%async_computation.1 | async-start | bytes 2359296 | tf_op jit(solution)/shard_map/all_to_all | solution.py:308
  136.2 0.8 broadcast_in_dim.2.scale_ref
  137.0 11.7 %inverse.2.done_ref = bf16[3,90,16,1440]{3,2,1,0:T(8,128)(2,1)} custom-call(f32[90,1,512]{2,1,0:T(1,128)} %broadcast_in_dim.2.scale_ref, bf16[1440,512]{1,0:T(8,128)(2,1)} %get-tuple-element.14.table_ref, bf16[32,2,144,128]{3,2,1,0:T(8,128)(2,1)} %all-to-all-done.3.x_ref), custom_call_target="tpu_custom_call" | custom-call | flops 8493465600 | bytes 12000000 | tf_op jit(solution)/shard_map/inverse/pallas_call | solution.py:263
  148.7 6.0 %all-to-all-done.1.x_ref = bf16[32,1,144,128]{3,2,1,0:T(8,128)(2,1)} async-done(((bf16[32,1,144,128]{3,2,1,0:T(8,128)(2,1)}), bf16[32,1,144,128]{3,2,1,0:T(8,128)(2,1)}, u32[]{:S(2)}, u32[]{:S(2)}) %all-to-all-start.1) | async-done | bytes 1179680 | tf_op jit(solution)/shard_map/all_to_all | solution.py:308
  154.7 7.7 %inverse.3 = bf16[3,90,16,1440]{3,2,1,0:T(8,128)(2,1)} custom-call(f32[90,1,512]{2,1,0:T(1,128)} %broadcast_in_dim.2.scale_ref, bf16[1440,512]{1,0:T(8,128)(2,1)} %get-tuple-element.14.table_ref, bf16[32,1,144,128]{3,2,1,0:T(8,128)(2,1)} %all-to-all-done.1.x_ref, bf16[3,90,16,1440]{3,2,1,0:T(8,128)(2,1)} %inverse.2.done_ref), custom_call_target="tpu_custom_call", output_to_operand_aliasing={{}: (3, {})} | custom-call | flops 4246732800 | bytes 6000000 | tf_op jit(solution)/shard_map/inverse/pallas_call | solution.py:263
  (38 shorter events, 3.9 us)
Async XLA Ops:
  0.0 10.5 %copy-start.6 = (s32[96]{0:T(128)S(1)}, s32[96]{0:T(128)}, u32[]{:S(2)}) copy-start(s32[96]{0:T(128)} %param.11) | copy-start | bytes 1156
  0.8 23.6 %collective-permute-start.3 = (f32[2,16,768]{2,1,0:T(8,128)S(1)}, f32[2,16,768]{2,1,0:T(8,128)}, u32[]{:S(2)}, u32[]{:S(2)}) collective-permute-start(f32[2,16,768]{2,1,0:T(8,128)S(1)} %select_maximum_fusion), channel_id=1, source_target_pairs={{0,8},{8,0},{1,9},{9,1},{2,10},{10,2},{3,11},{11,3},{4,12},{12,4},... | collective-permute-start | bytes 294920 | tf_op jit(solution)/shard_map/ppermute | solution.py:291
  6.6 17.8 %collective-permute-start.2 = (bf16[3,45,768]{2,1,0:T(8,128)(2,1)}, bf16[3,45,768]{2,1,0:T(8,128)(2,1)S(1)}, u32[]{:S(2)}, u32[]{:S(2)}) collective-permute-start(bf16[3,45,768]{2,1,0:T(8,128)(2,1)} %get-tuple-element.23), channel_id=1, source_target_pairs={{0,9},{1,8},{8,1},{9,0},{2,11},{3,10},{10,3},{11,2},{4,13},{5,12},... | collective-permute-start | bytes 622088 | tf_op jit(solution)/shard_map/ppermute | solution.py:289
  7.6 16.8 %collective-permute-start.1 = (bf16[3,45,768]{2,1,0:T(8,128)(2,1)}, bf16[3,45,768]{2,1,0:T(8,128)(2,1)S(1)}, u32[]{:S(2)}, u32[]{:S(2)}) collective-permute-start(bf16[3,45,768]{2,1,0:T(8,128)(2,1)} %get-tuple-element.24), channel_id=1, source_target_pairs={{0,8},{1,9},{8,0},{9,1},{2,10},{3,11},{10,2},{11,3},{4,12},{5,13},... | collective-permute-start | bytes 622088 | tf_op jit(solution)/shard_map/ppermute | solution.py:289
  10.4 14.0 %collective-permute-start = (bf16[3,45,768]{2,1,0:T(8,128)(2,1)S(1)}, bf16[3,45,768]{2,1,0:T(8,128)(2,1)S(1)}, u32[]{:S(2)}, u32[]{:S(2)}) collective-permute-start(bf16[3,45,768]{2,1,0:T(8,128)(2,1)S(1)} %get-tuple-element.25), channel_id=1, source_target_pairs={{0,1},{1,0},{8,9},{9,8},{2,3},{3,2},{10,11},{11,10},{4,5},{5,4},{1... | collective-permute-start | bytes 622088 | tf_op jit(solution)/shard_map/ppermute | solution.py:289
  24.4 0.7 copy-start.2
  24.5 0.8 copy-start.3
  24.5 0.8 copy-start.4
  24.5 6.6 %copy-start.1 = (bf16[3,45,768]{2,1,0:T(8,128)(2,1)S(1)}, bf16[3,45,768]{2,1,0:T(8,128)(2,1)}, u32[]{:S(2)}) copy-start(bf16[3,45,768]{2,1,0:T(8,128)(2,1)} %get-tuple-element.18) | copy-start | bytes 622084
  25.3 37.5 %all-to-all-start.2 = ((bf16[32,2,144,128]{3,2,1,0:T(8,128)(2,1)}), bf16[32,2,144,128]{3,2,1,0:T(8,128)(2,1)}, u32[]{:S(2)}, u32[]{:S(2)}) async-start(bf16[32,2,144,128]{3,2,1,0:T(8,128)(2,1)} %get-tuple-element.22), calls=%async_computation.2 | async-start | bytes 4718592 | tf_op jit(solution)/shard_map/all_to_all | solution.py:297
  32.3 12.4 %copy-start = (bf16[4,3,48,768]{3,2,1,0:T(8,128)(2,1)}, bf16[4,3,48,768]{3,2,1,0:T(8,128)(2,1)S(1)}, u32[]{:S(2)}) copy-start(bf16[4,3,48,768]{3,2,1,0:T(8,128)(2,1)S(1)} %fusion.6.t0) | copy-start | bytes 2654212
  32.3 41.5 %collective-permute-start.7 = (bf16[4,3,48,768]{3,2,1,0:T(8,128)(2,1)S(1)}, bf16[4,3,48,768]{3,2,1,0:T(8,128)(2,1)}, u32[]{:S(2)}, u32[]{:S(2)}) collective-permute-start(bf16[4,3,48,768]{3,2,1,0:T(8,128)(2,1)S(1)} %fusion.6.t0), channel_id=1, source_target_pairs={{0,6},{2,0},{4,2},{6,4},{1,7},{3,1},{5,3},{7,5},{8,14},{10,8},{12,... | collective-permute-start | bytes 2654216 | tf_op jit(solution)/shard_map/ppermute | solution.py:300
  36.1 37.7 %collective-permute-start.6 = (bf16[4,3,48,768]{3,2,1,0:T(8,128)(2,1)S(1)}, bf16[4,3,48,768]{3,2,1,0:T(8,128)(2,1)}, u32[]{:S(2)}, u32[]{:S(2)}) collective-permute-start(bf16[4,3,48,768]{3,2,1,0:T(8,128)(2,1)S(1)} %fusion.6.t0), channel_id=1, source_target_pairs={{0,4},{2,6},{4,0},{6,2},{1,5},{3,7},{5,1},{7,3},{8,12},{10,14},{12... | collective-permute-start | bytes 2654216 | tf_op jit(solution)/shard_map/ppermute | solution.py:300
  36.1 41.5 %collective-permute-start.5 = (bf16[4,3,48,768]{3,2,1,0:T(8,128)(2,1)S(1)}, bf16[4,3,48,768]{3,2,1,0:T(8,128)(2,1)}, u32[]{:S(2)}, u32[]{:S(2)}) collective-permute-start(bf16[4,3,48,768]{3,2,1,0:T(8,128)(2,1)S(1)} %fusion.6.t0), channel_id=1, source_target_pairs={{0,2},{2,4},{4,6},{6,0},{1,3},{3,5},{5,7},{7,1},{8,10},{10,12},{12... | collective-permute-start | bytes 2654216 | tf_op jit(solution)/shard_map/ppermute | solution.py:300
  44.7 25.2 %copy-start.7 = (s32[96]{0:T(128)S(1)}, s32[96]{0:T(128)}, u32[]{:S(2)}) copy-start(s32[96]{0:T(128)} %param.11) | copy-start | bytes 1156
  62.8 27.8 %all-to-all-start = ((bf16[32,1,144,128]{3,2,1,0:T(8,128)(2,1)}), bf16[32,1,144,128]{3,2,1,0:T(8,128)(2,1)}, u32[]{:S(2)}, u32[]{:S(2)}) async-start(bf16[32,1,144,128]{3,2,1,0:T(8,128)(2,1)} %forward.3), calls=%async_computation | async-start | bytes 2359296 | tf_op jit(solution)/shard_map/all_to_all | solution.py:303
  69.6 4.3 %copy-start.5 = (f32[2,2,16,768]{3,2,1,0:T(8,128)}, f32[2,2,16,768]{3,2,1,0:T(8,128)S(1)}, u32[]{:S(2)}) copy-start(f32[2,2,16,768]{3,2,1,0:T(8,128)S(1)} %pad_maximum_fusion.f0) | copy-start | bytes 589828
  69.6 1.6 collective-permute-start.4
  71.1 2.7 %copy-start.8 = (f32[2,2,16,768]{3,2,1,0:T(8,128)}, f32[2,2,16,768]{3,2,1,0:T(8,128)S(1)}, u32[]{:S(2)}) copy-start(f32[2,2,16,768]{3,2,1,0:T(8,128)S(1)} %collective-permute-done.4.f1) | copy-start | bytes 589828
  90.7 39.6 %all-to-all-start.3 = ((bf16[32,2,144,128]{3,2,1,0:T(8,128)(2,1)}), bf16[32,2,144,128]{3,2,1,0:T(8,128)(2,1)}, u32[]{:S(2)}, u32[]{:S(2)}) async-start(bf16[32,2,144,128]{3,2,1,0:T(8,128)(2,1)} %spectral.3), calls=%async_computation.3 | async-start | bytes 4718592 | tf_op jit(solution)/shard_map/all_to_all | solution.py:307
  109.2 27.0 %copy-start.9 = (f32[90]{0:T(128)S(1)}, f32[90]{0:T(128)}, u32[]{:S(2)}) copy-start(f32[90]{0:T(128)} %param.10) | copy-start | bytes 1084
  130.3 24.4 %all-to-all-start.1 = ((bf16[32,1,144,128]{3,2,1,0:T(8,128)(2,1)}), bf16[32,1,144,128]{3,2,1,0:T(8,128)(2,1)}, u32[]{:S(2)}, u32[]{:S(2)}) async-start(bf16[32,1,144,128]{3,2,1,0:T(8,128)(2,1)} %spectral.2), calls=%async_computation.1 | async-start | bytes 2359296 | tf_op jit(solution)/shard_map/all_to_all | solution.py:308

commit v2 on v1

v2 whole, which is shorter than its diff:
```python
import functools
import math

import jax
import jax.numpy as jnp
from jax import lax
from jax.experimental import pallas as pl
from jax.experimental.pallas import tpu as pltpu
from jax.sharding import Mesh
from jax.sharding import PartitionSpec as P

NLON = 1440
M = 720
ROWS = 768
PAIRS = 96
SAMPLES = 3
EARLY = 2
EXTRA = 8
CH = 16
LAT = 90
HALF = 45
HP = 48
DEST = 32
SLOTS = 3
GROUPS = 4
LANES = 128
COLS = 4 * LANES
STEP = 16
CHUNK = 9
VMEM = 63 * 1024 * 1024

SLOT_AXES = ("x_lo", "y", "x_hi", "core")
NT = (((1,), (1,)), ((), ()))
TN = (((0,), (0,)), ((), ()))


def packed_rows(count):
    return (SLOTS * count * HALF + 7) // 8 * 8


def fill_table(low, table, coarse_cos, coarse_sin):
    orders = jnp.concatenate([low, M - 1 - low], axis=1)
    unit = 2.0 * math.pi / NLON

    def angle(count, scale):
        k = lax.broadcasted_iota(jnp.int32, (count, 2 * LANES), 0) * scale
        return lax.rem(k * orders, NLON).astype(jnp.float32) * unit

    coarse = angle(96, STEP)
    coarse_cos[...] = jnp.cos(coarse)
    coarse_sin[...] = jnp.sin(coarse)
    fine = angle(STEP, 1)
    fine_cos, fine_sin = jnp.cos(fine), jnp.sin(fine)

    @pl.loop(0, NLON // STEP)
    def _(a):
        base_cos, base_sin = coarse_cos[pl.ds(a, 1), :], coarse_sin[pl.ds(a, 1), :]
        even = (base_cos * fine_cos - base_sin * fine_sin).astype(table.dtype)
        odd = (-(base_sin * fine_cos) - base_cos * fine_sin).astype(table.dtype)
        rows = pl.ds(pl.multiple_of(a * STEP, STEP), STEP)
        table[rows, :LANES] = even[:, :LANES]
        table[rows, LANES : 2 * LANES] = odd[:, :LANES]
        table[rows, 2 * LANES : 3 * LANES] = even[:, LANES:]
        table[rows, 3 * LANES :] = odd[:, LANES:]


def first_forward_kernel(low_ref, x_ref, out_ref, table_ref, product, packed, coarse_cos, coarse_sin):
    @pl.when((pl.program_id(0) == 0) & (pl.program_id(1) == 0))
    def _():
        fill_table(low_ref[...], table_ref, coarse_cos, coarse_sin)
        packed[...] = jnp.zeros_like(packed)

    transform(low_ref, x_ref, table_ref, out_ref, product, packed)


def later_forward_kernel(low_ref, x_ref, table_ref, out_ref, product, packed):
    @pl.when((pl.program_id(0) == 0) & (pl.program_id(1) == 0))
    def _():
        packed[...] = jnp.zeros_like(packed)

    transform(low_ref, x_ref, table_ref, out_ref, product, packed)


def transform(low_ref, x_ref, table_ref, out_ref, product, packed):
    sample, count = pl.program_id(0), pl.num_programs(0)
    rows_each = out_ref.shape[1]
    factor = jnp.where(low_ref[...] == 0, 1.0, 2.0).astype(jnp.float32)

    block = x_ref[0].reshape(HALF * CH, NLON)
    rows = pl.ds(pl.multiple_of(pl.program_id(1) * HALF * CH, CH), HALF * CH)
    product[rows, :] = jnp.dot(block, table_ref[...], preferred_element_type=jnp.float32)

    @pl.when(pl.program_id(1) == 1)
    def _():
        @pl.loop(0, HALF // CHUNK)
        def _(step):
            first = step * CHUNK
            for t in range(CHUNK):
                pieces = []
                for q in range(4):
                    scale = factor if q < 2 else 2.0
                    for half in range(2):
                        rows = pl.ds(pl.multiple_of((half * HALF + first + t) * CH, CH), CH)
                        pieces.append(product[rows, q * LANES : (q + 1) * LANES] * scale)
                turned = jnp.concatenate(pieces, axis=0).T
                for slot in range(SLOTS):
                    row = (slot * count + sample) * HALF + first + t
                    packed[pl.ds(row, DEST, stride=rows_each), :] = turned[slot * DEST : (slot + 1) * DEST]

    @pl.when((sample == count - 1) & (pl.program_id(1) == 1))
    def _():
        for device in range(DEST):
            out_ref[device] = packed[device * rows_each : (device + 1) * rows_each, :].astype(out_ref.dtype)


def forward(low, grad, start, count, table=None):
    whole = pl.BlockSpec((NLON, COLS), lambda s, half: (0, 0))
    in_specs = [
        pl.BlockSpec((1, LANES), lambda s, half: (0, 0)),
        pl.BlockSpec((1, HALF, CH, NLON), lambda s, half: (s + start, half, 0, 0)),
    ]
    shape = (DEST, packed_rows(count), LANES)
    out_specs = [pl.BlockSpec(shape, lambda s, half: (0, 0, 0))]
    out_shape = [jax.ShapeDtypeStruct(shape, jnp.bfloat16)]
    scratch = [pltpu.VMEM((LAT * CH, COLS), jnp.float32), pltpu.VMEM((DEST * packed_rows(count), LANES), jnp.float32)]
    if table is None:
        out_specs.append(whole)
        out_shape.append(jax.ShapeDtypeStruct((NLON, COLS), jnp.bfloat16))
        scratch += [pltpu.VMEM((96, 2 * LANES), jnp.float32)] * 2
    else:
        in_specs.append(whole)
    return pl.pallas_call(
        first_forward_kernel if table is None else later_forward_kernel,
        grid=(count, 2),
        in_specs=in_specs,
        out_specs=out_specs,
        out_shape=out_shape,
        scratch_shapes=scratch,
        compiler_params=pltpu.CompilerParams(vmem_limit_bytes=VMEM),
        cost_estimate=pl.CostEstimate(flops=4 * count * 1440 * NLON * COLS, bytes_accessed=count * 6_000_000, transcendentals=0),
        name="forward",
    )(low, grad, *([] if table is None else [table]))


def spectral_kernel(count, low_ref, place_ref, f0, f1, x_ref, t0, t1, t2, t3, out_ref, legendre, columns, split, synthesis, gains, wide, sems):
    slot = pl.program_id(0)
    group, z = place_ref[0], place_ref[1]

    rows_each = x_ref.shape[1]

    def table_copies(which):
        copies = []
        for other in range(GROUPS):
            for shift, source in enumerate((t0, t1, t2, t3)):
                block = other // 2 * 8 + lax.rem(z + (4 - shift), 4) * 2 + other % 2
                copies.append(pltpu.make_async_copy(source.at[other, which], legendre.at[which, block], sems.at[which, other * 4 + shift]))
        return copies

    @pl.when(slot == 0)
    def _():
        for which in range(SLOTS):
            for copy in table_copies(which):
                copy.start()
        for device in range(DEST):
            wide[device * rows_each : (device + 1) * rows_each, :] = x_ref[device].astype(jnp.float32)
        wide[DEST * rows_each :, :] = jnp.zeros((EXTRA, LANES), jnp.float32)

    low = low_ref[slot]
    below = lax.broadcasted_iota(jnp.int32, (1, ROWS), 1) < M - low
    for k in range(GROUPS):
        rows = pl.ds(pl.multiple_of(jnp.bitwise_xor(group, k) * CH, CH), CH)
        for part in range(2):
            whole = (f1 if k % 2 else f0)[k // 2, part]
            gains[part, rows, :] = jnp.where(below, pltpu.roll(whole, ROWS - low, 1), pltpu.roll(whole, 1, 1))

    lane = lax.broadcasted_iota(jnp.int32, (HP, LANES), 1)
    former_half = lax.rem(lax.div(lane, CH), 2) == 0

    def shuffle(a, b):
        return jnp.where(former_half, a, pltpu.roll(b, CH, 1)), jnp.where(former_half, pltpu.roll(a, LANES - CH, 1), b)

    tiles = [(sample, pair, slice((sample * 2 + pair) * LANES, (sample * 2 + pair + 1) * LANES)) for sample in range(count) for pair in range(2)]

    def place(order, pair, offset, sample):
        return (order * GROUPS + pair * 2 + offset) * rows_each + (slot * count + sample) * HALF

    @pl.loop(0, 8)
    def _(order):
        for sample, pair, lanes in tiles:
            a, b = (wide[pl.ds(place(order, pair, offset, sample), HP), :] for offset in range(2))
            for half, value in enumerate(shuffle(a, b)):
                rows = pl.ds(pl.multiple_of((order * 2 + half) * HP, HP), HP)
                columns[rows, lanes] = value.astype(columns.dtype)

    for copy in table_copies(slot):
        copy.wait()
    table = legendre[slot].reshape(16 * HP, ROWS)
    spectrum = lax.dot_general(columns[...], table, TN, preferred_element_type=jnp.float32)
    for sample, pair, lanes in tiles:
        a0, a1, a2, a3 = (spectrum[lanes.start + q * 32 : lanes.start + (q + 1) * 32] for q in range(4))
        former, latter = jnp.where(below, a0, a2), jnp.where(below, a1, a3)
        re = gains[0, pair * 32 : (pair + 1) * 32]
        im = gains[1, pair * 32 : (pair + 1) * 32]
        real, imag = re * former + im * latter, re * latter - im * former
        parts = (jnp.where(below, real, 0.0), jnp.where(below, imag, 0.0), jnp.where(below, 0.0, real), jnp.where(below, 0.0, imag))
        for q in range(4):
            split[lanes.start + q * 32 : lanes.start + (q + 1) * 32, :] = parts[q].astype(split.dtype)
    synthesis[...] = lax.dot_general(table, split[...], NT, preferred_element_type=jnp.float32)

    @pl.loop(0, 8)
    def _(order):
        for sample, pair, lanes in tiles:
            halves = [synthesis[pl.ds(pl.multiple_of((order * 2 + half) * HP, HP), HP), lanes] for half in range(2)]
            for offset, value in enumerate(shuffle(*halves)):
                wide[pl.ds(place(order, pair, offset, sample), HALF), :] = value[:HALF]

    @pl.when(slot == SLOTS - 1)
    def _():
        for device in range(DEST):
            out_ref[device] = wide[device * rows_each : (device + 1) * rows_each, :].astype(out_ref.dtype)


def spectral(low, place, filters, received, tables, count):
    width = count * 2 * LANES
    block = pl.BlockSpec(received.shape, lambda slot: (0, 0, 0))
    smem = pl.BlockSpec(memory_space=pltpu.SMEM)
    hbm = pl.BlockSpec(memory_space=pl.ANY)
    gain = pl.BlockSpec((2, 2, CH, ROWS), lambda slot: (0, 0, 0, 0))
    return pl.pallas_call(
        functools.partial(spectral_kernel, count),
        grid=(SLOTS,),
        in_specs=[smem, smem] + [gain] * 2 + [block] + [hbm] * 4,
        out_specs=block,
        out_shape=jax.ShapeDtypeStruct(received.shape, jnp.bfloat16),
        scratch_shapes=[
            pltpu.VMEM((SLOTS, 16, HP, ROWS), jnp.bfloat16),
            pltpu.VMEM((16 * HP, width), jnp.bfloat16),
            pltpu.VMEM((width, ROWS), jnp.bfloat16),
            pltpu.VMEM((16 * HP, width), jnp.float32),
            pltpu.VMEM((2, GROUPS * CH, ROWS), jnp.float32),
            pltpu.VMEM((DEST * packed_rows(count) + EXTRA, LANES), jnp.float32),
            pltpu.SemaphoreType.DMA((SLOTS, 16)),
        ],
        compiler_params=pltpu.CompilerParams(vmem_limit_bytes=VMEM),
        cost_estimate=pl.CostEstimate(flops=12 * ROWS * ROWS * width, bytes_accessed=12_000_000, transcendentals=0),
        name="spectral",
    )(low, place, *filters, received, *tables)


def later_inverse_kernel(scale_ref, table_ref, x_ref, done_ref, out_ref, packed, left):
    inverse_kernel(scale_ref, table_ref, x_ref, out_ref, packed, left)


def inverse_kernel(scale_ref, table_ref, x_ref, out_ref, packed, left):
    sample, count = pl.program_id(0), pl.num_programs(0)
    rows_each = x_ref.shape[1]

    @pl.when((sample == 0) & (pl.program_id(1) == 0))
    def _():
        for device in range(DEST):
            packed[device * rows_each : (device + 1) * rows_each, :] = x_ref[device].astype(jnp.float32)

    blank = jnp.zeros((LANES - PAIRS, LANES), jnp.float32)

    @pl.when(pl.program_id(1) == 0)
    def _():
        @pl.loop(0, HALF // CHUNK)
        def _(step):
            first = step * CHUNK
            for t in range(CHUNK):
                starts = [(slot * count + sample) * HALF + first + t for slot in range(SLOTS)]
                pieces = [packed[pl.ds(start, DEST, stride=rows_each), :] for start in starts]
                turned = jnp.concatenate(pieces + [blank], axis=0).T.astype(left.dtype)
                for q in range(4):
                    for half in range(2):
                        piece = turned[(q * 2 + half) * CH : (q * 2 + half + 1) * CH]
                        rows = pl.ds(pl.multiple_of((half * HALF + first + t) * CH, CH), CH)
                        left[rows, q * LANES : (q + 1) * LANES] = piece

    rows = pl.ds(pl.multiple_of(pl.program_id(1) * HALF * CH, CH), HALF * CH)
    for start in range(0, NLON, 512):
        stop = min(start + 512, NLON)
        values = lax.dot_general(left[rows, :], table_ref[start:stop, :], NT, preferred_element_type=jnp.float32)
        values = values.reshape(HALF, CH, stop - start) * scale_ref[:, :, : stop - start]
        out_ref[0, :, :, start:stop] = values.astype(out_ref.dtype)


def inverse(scale, table, received, start, count, done=None):
    in_specs = [
        pl.BlockSpec((HALF, 1, 512), lambda s, half: (half, 0, 0)),
        pl.BlockSpec((NLON, COLS), lambda s, half: (0, 0)),
        pl.BlockSpec(received.shape, lambda s, half: (0, 0, 0)),
    ]
    return pl.pallas_call(
        inverse_kernel if done is None else later_inverse_kernel,
        grid=(count, 2),
        in_specs=in_specs if done is None else in_specs + [pl.BlockSpec(memory_space=pl.ANY)],
        out_specs=pl.BlockSpec((1, HALF, CH, NLON), lambda s, half: (s + start, half, 0, 0)),
        out_shape=jax.ShapeDtypeStruct((SAMPLES, LAT, CH, NLON), jnp.bfloat16),
        input_output_aliases={} if done is None else {3: 0},
        scratch_shapes=[
            pltpu.VMEM((DEST * received.shape[1], LANES), jnp.float32),
            pltpu.VMEM((LAT * CH, COLS), jnp.bfloat16),
        ],
        compiler_params=pltpu.CompilerParams(vmem_limit_bytes=VMEM),
        cost_estimate=pl.CostEstimate(flops=4 * count * 1440 * NLON * COLS, bytes_accessed=count * 6_000_000, transcendentals=0),
        name="inverse",
    )(scale, table, received, *([] if done is None else [done]))


def body(grad_out, legendre, filter_re, filter_im, quad_weight, pair_order):
    group = lax.axis_index("x_hi") * 2 + lax.axis_index("core")
    z = lax.axis_index("z")
    mine = (lax.axis_index("x_lo") * 4 + lax.axis_index("y")) * GROUPS + group

    own = lax.all_to_all(legendre.reshape(GROUPS, SLOTS, HALF, ROWS), ("x_hi", "core"), 0, 0)

    filters = jnp.pad(jnp.stack([filter_re, filter_im]), ((0, 0), (0, 0), (0, ROWS - M)))
    far = lax.ppermute(filters, "x_hi", [(0, 1), (1, 0)])

    low_lanes = jnp.pad(pair_order.reshape(DEST, SLOTS).T.reshape(1, PAIRS), ((0, 0), (0, LANES - PAIRS)))
    grad = jnp.transpose(grad_out, (0, 2, 1, 3))
    packed, table = forward(low_lanes, grad, 0, EARLY)
    packed, own, far = lax.optimization_barrier((packed, own, far))
    early = lax.all_to_all(packed, SLOT_AXES, 0, 0)
    own = jnp.pad(own, ((0, 0), (0, 0), (0, HP - HALF), (0, 0)))
    tables = [own] + [lax.ppermute(own, "z", [(i, (i + shift) % 4) for i in range(4)]) for shift in range(1, 4)]
    (packed,) = forward(low_lanes, grad, EARLY, SAMPLES - EARLY, table)
    late = lax.all_to_all(packed, SLOT_AXES, 0, 0)
    near = jnp.stack([filters, far])
    filters = [near, lax.ppermute(near, "core", [(0, 1), (1, 0)])]

    low = lax.dynamic_slice_in_dim(pair_order, mine * SLOTS, SLOTS)
    place = jnp.stack([group, z])
    early = lax.all_to_all(spectral(low, place, filters, early, tables, EARLY), SLOT_AXES, 0, 0)
    late = lax.all_to_all(spectral(low, place, filters, late, tables, SAMPLES - EARLY), SLOT_AXES, 0, 0)

    scale = jnp.broadcast_to((quad_weight * (2.0 * math.pi / NLON))[:, None, None], (LAT, 1, 512))
    values = inverse(scale, table, early, 0, EARLY)
    values = inverse(scale, table, late, EARLY, SAMPLES - EARLY, values)
    return jnp.transpose(values, (0, 2, 1, 3))


def solution(mesh):
    fine = Mesh(mesh.devices.reshape(2, 4, 2, 4, 2), ("x_lo", "y", "x_hi", "z", "core"))
    order, chan = ("x_lo", "y"), ("x_hi", "z", "core")
    in_specs = (P(None, chan, order, None), P(order, chan, None), P(chan, None), P(chan, None), P(order), P())
    return jax.shard_map(body, mesh=fine, in_specs=in_specs, out_specs=P(None, chan, order, None), check_vma=False)
```

time: 163 us -> 162 us (level)
  waiting for transfers between devices: 51.7 us -> 49.3 us
  starting transfers between devices: 37.7 us -> 39.4 us
    all_to_all x2 -> x3, starting transfers between devices: 13.7 us -> 20 us  [the longest x1 7.86 us: body(): lax.all_to_all(spectral(low, place, filters, early, tables, EARLY), SLOT_...]
    ppermute x4 -> x1, starting transfers between devices: 7.47 us -> 2.89 us  [body(): far = lax.ppermute(filters, 'x_hi', [(0, 1), (1, 0)])]
    all_to_all x2 -> x3, waiting for transfers between devices: 27.1 us -> 24.2 us  [the longest x1 18.6 us: body(): lax.all_to_all(spectral(low, place, filters, early, tables, EARLY), SLOT_...]
    pallas_call x2, Pallas kernels: 23.6 us -> 26.4 us  [spectral(): pl.pallas_call(functools.partial(spectral_kernel, count), grid=(SLOTS,),...]
    squeeze x1 -> x0, local copies, waits for them, and re-layouts: 2.13 us -> none  [body(): lax.dynamic_index_in_dim(by_group, jnp.bitwise_xor(group, k), 0, keepdims...]
  transfers between devices with their start and end apart: 12 -> 10, of which waited for: 5 -> 5; matrix products, arithmetic and copies ran while one was open for 4% -> 4% of each run, Pallas kernels for 35% -> 36%
where the time goes in v2:
time: 162 us; the launch traced here: 161 us
  Pallas kernels  65 us (40%)
  waiting for transfers between devices  49.3 us (30%)
  starting transfers between devices  39.4 us (24%)
  local copies, waits for them, and re-layouts  3.97 us (2%)
  other arithmetic  3.04 us (2%)
    pallas_call x2, Pallas kernels, spectral(): pl.pallas_call(functools.partial(spectral_kernel, count), grid=(SLOTS,),...  26.4 us
    pallas_call x2, Pallas kernels, forward(): pl.pallas_call(first_forward_kernel if table is None else later_forward_k...  20.4 us
    all_to_all x1, waiting for transfers between devices, body(): lax.all_to_all(spectral(low, place, filters, early, tables, EARLY), SLOT_...  18.6 us
    pallas_call x2, Pallas kernels, inverse(): pl.pallas_call(inverse_kernel if done is None else later_inverse_kernel,...  18.2 us
    all_to_all x1, waiting for transfers between devices, body(): early = lax.all_to_all(packed, SLOT_AXES, 0, 0)  17.6 us
    all_to_all x1, starting transfers between devices, body(): lax.all_to_all(spectral(low, place, filters, early, tables, EARLY), SLOT_...  7.86 us
    ppermute x3, waiting for transfers between devices, body(): lax.ppermute(own, 'z', [(i, (i + shift) % 4) for i in range(4)])  7.37 us
    all_to_all x1, starting transfers between devices, body(): lax.all_to_all(spectral(low, place, filters, late, tables, SAMPLES - EARL...  6.32 us
  transfers between devices with their start and end apart: 10, of which 5 were waited for; matrix products, arithmetic and copies ran while one was open for 4% of the time, Pallas kernels for 36%

profile of v2, /device:TPU:1, one launch (start us, length us, event | category | flops | bytes accessed | tf_op | source)
XLA Modules:
  0.0 160.8 jit_solution(14896674642253736162)
XLA Ops:
  0.0 5.8 %all-to-all-start = ((bf16[4,3,45,768]{3,2,1,0:T(8,128)(2,1)}), bf16[4,3,45,768]{3,2,1,0:T(8,128)(2,1)S(1)}, u32[]{:S(2)}, u32[]{:S(2)}) async-start(bf16[4,3,45,768]{3,2,1,0:T(8,128)(2,1)} %bitcast.13), calls=%async_computation | async-start | bytes 1769472 | tf_op jit(solution)/shard_map/all_to_all | solution.py:316
  5.8 1.5 fusion
  7.3 2.9 %collective-permute-start = (f32[2,16,768]{2,1,0:T(8,128)}, f32[2,16,768]{2,1,0:T(8,128)}, u32[]{:S(2)}, u32[]{:S(2)}) collective-permute-start(f32[2,16,768]{2,1,0:T(8,128)} %get-tuple-element.16), channel_id=1, source_target_pairs={{0,8},{8,0},{1,9},{9,1},{2,10},{10,2},{3,11},{11,3},{4,12},{12,4},... | collective-permute-start | bytes 294920 | tf_op jit(solution)/shard_map/ppermute | solution.py:319
  10.2 0.7 reshape.12
  11.7 13.3 %forward.2 = (bf16[32,272,128]{2,1,0:T(8,128)(2,1)}, bf16[1440,512]{1,0:T(8,128)(2,1)}) custom-call(s32[1,128]{1,0:T(1,128)} %pad.12.low_ref, bf16[3,90,16,1440]{3,2,1,0:T(8,128)(2,1)} %bitcast.11), custom_call_target="tpu_custom_call" | custom-call | flops 8493465600 | bytes 12000000 | tf_op jit(solution)/shard_map/forward/pallas_call | solution.py:132
  25.0 5.4 %all-to-all-start.3 = ((bf16[32,272,128]{2,1,0:T(8,128)(2,1)}), bf16[32,272,128]{2,1,0:T(8,128)(2,1)}, u32[]{:S(2)}, u32[]{:S(2)}) async-start(bf16[32,272,128]{2,1,0:T(8,128)(2,1)} %get-tuple-element.14), calls=%async_computation.3 | async-start | bytes 4456448 | tf_op jit(solution)/shard_map/all_to_all | solution.py:325
  30.5 1.0 pad.14.t0
  31.4 3.8 %collective-permute-start.4 = (bf16[4,3,48,768]{3,2,1,0:T(8,128)(2,1)}, bf16[4,3,48,768]{3,2,1,0:T(8,128)(2,1)}, u32[]{:S(2)}, u32[]{:S(2)}) collective-permute-start(bf16[4,3,48,768]{3,2,1,0:T(8,128)(2,1)} %pad.14.t0), channel_id=1, source_target_pairs={{0,6},{2,0},{4,2},{6,4},{1,7},{3,1},{5,3},{7,5},{8,14},{10,8},{12,... | collective-permute-start | bytes 2654216 | tf_op jit(solution)/shard_map/ppermute | solution.py:327
  35.2 0.7 collective-permute-start.2
  35.9 7.1 %forward.3 = bf16[32,136,128]{2,1,0:T(8,128)(2,1)} custom-call(s32[1,128]{1,0:T(1,128)} %pad.12.low_ref, bf16[3,90,16,1440]{3,2,1,0:T(8,128)(2,1)} %bitcast.12, bf16[1440,512]{1,0:T(8,128)(2,1)} %get-tuple-element.10.table_ref), custom_call_target="tpu_custom_call" | custom-call | flops 4246732800 | bytes 6000000 | tf_op jit(solution)/shard_map/forward/pallas_call | solution.py:132
  43.0 17.6 %all-to-all-done.3.x_ref = bf16[32,272,128]{2,1,0:T(8,128)(2,1)} async-done(((bf16[32,272,128]{2,1,0:T(8,128)(2,1)}), bf16[32,272,128]{2,1,0:T(8,128)(2,1)}, u32[]{:S(2)}, u32[]{:S(2)}) %all-to-all-start.3) | async-done | bytes 2228256 | tf_op jit(solution)/shard_map/all_to_all | solution.py:325
  60.6 6.3 %all-to-all-start.1 = ((bf16[32,136,128]{2,1,0:T(8,128)(2,1)}), bf16[32,136,128]{2,1,0:T(8,128)(2,1)}, u32[]{:S(2)}, u32[]{:S(2)}) async-start(bf16[32,136,128]{2,1,0:T(8,128)(2,1)} %forward.3), calls=%async_computation.1 | async-start | bytes 2228224 | tf_op jit(solution)/shard_map/all_to_all | solution.py:329
  67.0 0.9 pad_maximum_fusion.f0
  69.6 3.6 %collective-permute-done.4.t3 = bf16[4,3,48,768]{3,2,1,0:T(8,128)(2,1)} collective-permute-done((bf16[4,3,48,768]{3,2,1,0:T(8,128)(2,1)}, bf16[4,3,48,768]{3,2,1,0:T(8,128)(2,1)}, u32[]{:S(2)}, u32[]{:S(2)}) %collective-permute-start.4) | collective-permute-done | bytes 884768 | tf_op jit(solution)/shard_map/ppermute | solution.py:327
  73.2 3.7 %collective-permute-done.2.t1 = bf16[4,3,48,768]{3,2,1,0:T(8,128)(2,1)} collective-permute-done((bf16[4,3,48,768]{3,2,1,0:T(8,128)(2,1)}, bf16[4,3,48,768]{3,2,1,0:T(8,128)(2,1)}, u32[]{:S(2)}, u32[]{:S(2)}) %collective-permute-start.2) | collective-permute-done | bytes 884768 | tf_op jit(solution)/shard_map/ppermute | solution.py:327
  77.0 14.8 %spectral.3 = bf16[32,272,128]{2,1,0:T(8,128)(2,1)} custom-call(s32[3]{0:T(128)} %dynamic_slice.3.low_ref, s32[2]{0:T(128)} %pad_add_fusion.place_ref, f32[2,2,16,768]{3,2,1,0:T(8,128)} %copy-done, f32[2,2,16,768]{3,2,1,0:T(8,128)} %copy-done.2, bf16[32,272,128]{2,1,0:T(8,128)(2,1)} %all-to-all-done.3.x_ref, bf16[4,3,48,768]{3,2,1,0:T(8,128)(2,1)} %pad.14.t0, ...), custom_call_target="tpu_custom_call" | custom-call | flops 3623878656 | bytes 12000000 | tf_op jit(solution)/shard_map/spectral/pallas_call | solution.py:229
  91.8 7.9 %all-to-all-start.4 = ((bf16[32,272,128]{2,1,0:T(8,128)(2,1)}), bf16[32,272,128]{2,1,0:T(8,128)(2,1)}, u32[]{:S(2)}, u32[]{:S(2)}) async-start(bf16[32,272,128]{2,1,0:T(8,128)(2,1)} %spectral.3), calls=%async_computation.4 | async-start | bytes 4456448 | tf_op jit(solution)/shard_map/all_to_all | solution.py:335
  99.7 11.5 %spectral.2 = bf16[32,136,128]{2,1,0:T(8,128)(2,1)} custom-call(s32[3]{0:T(128)} %dynamic_slice.3.low_ref, s32[2]{0:T(128)} %pad_add_fusion.place_ref, f32[2,2,16,768]{3,2,1,0:T(8,128)} %copy-done, f32[2,2,16,768]{3,2,1,0:T(8,128)} %copy-done.2, bf16[32,136,128]{2,1,0:T(8,128)(2,1)} %all-to-all-done.1.x_ref, bf16[4,3,48,768]{3,2,1,0:T(8,128)(2,1)} %pad.14.t0, ...), custom_call_target="tpu_custom_call" | custom-call | flops 1811939328 | bytes 12000000 | tf_op jit(solution)/shard_map/spectral/pallas_call | solution.py:229
  111.2 18.6 %all-to-all-done.4.x_ref = bf16[32,272,128]{2,1,0:T(8,128)(2,1)} async-done(((bf16[32,272,128]{2,1,0:T(8,128)(2,1)}), bf16[32,272,128]{2,1,0:T(8,128)(2,1)}, u32[]{:S(2)}, u32[]{:S(2)}) %all-to-all-start.4) | async-done | bytes 2228256 | tf_op jit(solution)/shard_map/all_to_all | solution.py:335
  129.8 6.3 %all-to-all-start.2 = ((bf16[32,136,128]{2,1,0:T(8,128)(2,1)}), bf16[32,136,128]{2,1,0:T(8,128)(2,1)}, u32[]{:S(2)}, u32[]{:S(2)}) async-start(bf16[32,136,128]{2,1,0:T(8,128)(2,1)} %spectral.2), calls=%async_computation.2 | async-start | bytes 2228224 | tf_op jit(solution)/shard_map/all_to_all | solution.py:336
  136.2 0.8 broadcast_in_dim.2.scale_ref
  137.0 11.4 %inverse.2.done_ref = bf16[3,90,16,1440]{3,2,1,0:T(8,128)(2,1)} custom-call(f32[90,1,512]{2,1,0:T(1,128)} %broadcast_in_dim.2.scale_ref, bf16[1440,512]{1,0:T(8,128)(2,1)} %get-tuple-element.10.table_ref, bf16[32,272,128]{2,1,0:T(8,128)(2,1)} %all-to-all-done.4.x_ref), custom_call_target="tpu_custom_call" | custom-call | flops 8493465600 | bytes 12000000 | tf_op jit(solution)/shard_map/inverse/pallas_call | solution.py:294
  148.4 5.6 %all-to-all-done.2.x_ref = bf16[32,136,128]{2,1,0:T(8,128)(2,1)} async-done(((bf16[32,136,128]{2,1,0:T(8,128)(2,1)}), bf16[32,136,128]{2,1,0:T(8,128)(2,1)}, u32[]{:S(2)}, u32[]{:S(2)}) %all-to-all-start.2) | async-done | bytes 1114144 | tf_op jit(solution)/shard_map/all_to_all | solution.py:336
  154.0 6.8 %inverse.3 = bf16[3,90,16,1440]{3,2,1,0:T(8,128)(2,1)} custom-call(f32[90,1,512]{2,1,0:T(1,128)} %broadcast_in_dim.2.scale_ref, bf16[1440,512]{1,0:T(8,128)(2,1)} %get-tuple-element.10.table_ref, bf16[32,136,128]{2,1,0:T(8,128)(2,1)} %all-to-all-done.2.x_ref, bf16[3,90,16,1440]{3,2,1,0:T(8,128)(2,1)} %inverse.2.done_ref), custom_call_target="tpu_custom_call", output_to_operand_aliasing={{}: (3, {})} | custom-call | flops 4246732800 | bytes 6000000 | tf_op jit(solution)/shard_map/inverse/pallas_call | solution.py:294
  (21 shorter events, 2.5 us)
Async XLA Ops:
  0.0 25.0 %all-to-all-start = ((bf16[4,3,45,768]{3,2,1,0:T(8,128)(2,1)}), bf16[4,3,45,768]{3,2,1,0:T(8,128)(2,1)S(1)}, u32[]{:S(2)}, u32[]{:S(2)}) async-start(bf16[4,3,45,768]{3,2,1,0:T(8,128)(2,1)} %bitcast.13), calls=%async_computation | async-start | bytes 1769472 | tf_op jit(solution)/shard_map/all_to_all | solution.py:316
  7.3 17.7 %collective-permute-start = (f32[2,16,768]{2,1,0:T(8,128)}, f32[2,16,768]{2,1,0:T(8,128)}, u32[]{:S(2)}, u32[]{:S(2)}) collective-permute-start(f32[2,16,768]{2,1,0:T(8,128)} %get-tuple-element.16), channel_id=1, source_target_pairs={{0,8},{8,0},{1,9},{9,1},{2,10},{10,2},{3,11},{11,3},{4,12},{12,4},... | collective-permute-start | bytes 294920 | tf_op jit(solution)/shard_map/ppermute | solution.py:319
  25.0 35.6 %all-to-all-start.3 = ((bf16[32,272,128]{2,1,0:T(8,128)(2,1)}), bf16[32,272,128]{2,1,0:T(8,128)(2,1)}, u32[]{:S(2)}, u32[]{:S(2)}) async-start(bf16[32,272,128]{2,1,0:T(8,128)(2,1)} %get-tuple-element.14), calls=%async_computation.3 | async-start | bytes 4456448 | tf_op jit(solution)/shard_map/all_to_all | solution.py:325
  31.4 41.8 %collective-permute-start.4 = (bf16[4,3,48,768]{3,2,1,0:T(8,128)(2,1)}, bf16[4,3,48,768]{3,2,1,0:T(8,128)(2,1)}, u32[]{:S(2)}, u32[]{:S(2)}) collective-permute-start(bf16[4,3,48,768]{3,2,1,0:T(8,128)(2,1)} %pad.14.t0), channel_id=1, source_target_pairs={{0,6},{2,0},{4,2},{6,4},{1,7},{3,1},{5,3},{7,5},{8,14},{10,8},{12,... | collective-permute-start | bytes 2654216 | tf_op jit(solution)/shard_map/ppermute | solution.py:327
  35.2 38.0 %collective-permute-start.3 = (bf16[4,3,48,768]{3,2,1,0:T(8,128)(2,1)}, bf16[4,3,48,768]{3,2,1,0:T(8,128)(2,1)}, u32[]{:S(2)}, u32[]{:S(2)}) collective-permute-start(bf16[4,3,48,768]{3,2,1,0:T(8,128)(2,1)} %pad.14.t0), channel_id=1, source_target_pairs={{0,4},{2,6},{4,0},{6,2},{1,5},{3,7},{5,1},{7,3},{8,12},{10,14},{12... | collective-permute-start | bytes 2654216 | tf_op jit(solution)/shard_map/ppermute | solution.py:327
  35.2 41.8 %collective-permute-start.2 = (bf16[4,3,48,768]{3,2,1,0:T(8,128)(2,1)}, bf16[4,3,48,768]{3,2,1,0:T(8,128)(2,1)}, u32[]{:S(2)}, u32[]{:S(2)}) collective-permute-start(bf16[4,3,48,768]{3,2,1,0:T(8,128)(2,1)} %pad.14.t0), channel_id=1, source_target_pairs={{0,2},{2,4},{4,6},{6,0},{1,3},{3,5},{5,7},{7,1},{8,10},{10,12},{12... | collective-permute-start | bytes 2654216 | tf_op jit(solution)/shard_map/ppermute | solution.py:327
  43.0 25.3 %copy-start.1 = (s32[96]{0:T(128)S(1)}, s32[96]{0:T(128)}, u32[]{:S(2)}) copy-start(s32[96]{0:T(128)} %param.11) | copy-start | bytes 1156
  60.6 31.2 %all-to-all-start.1 = ((bf16[32,136,128]{2,1,0:T(8,128)(2,1)}), bf16[32,136,128]{2,1,0:T(8,128)(2,1)}, u32[]{:S(2)}, u32[]{:S(2)}) async-start(bf16[32,136,128]{2,1,0:T(8,128)(2,1)} %forward.3), calls=%async_computation.1 | async-start | bytes 2228224 | tf_op jit(solution)/shard_map/all_to_all | solution.py:329
  67.9 9.1 %copy-start = (f32[2,2,16,768]{3,2,1,0:T(8,128)}, f32[2,2,16,768]{3,2,1,0:T(8,128)S(1)}, u32[]{:S(2)}) copy-start(f32[2,2,16,768]{3,2,1,0:T(8,128)S(1)} %pad_maximum_fusion.f0) | copy-start | bytes 589828
  67.9 1.7 %collective-permute-start.1 = (f32[2,2,16,768]{3,2,1,0:T(8,128)S(1)}, f32[2,2,16,768]{3,2,1,0:T(8,128)S(1)}, u32[]{:S(2)}, u32[]{:S(2)}) collective-permute-start(f32[2,2,16,768]{3,2,1,0:T(8,128)S(1)} %pad_maximum_fusion.f0), channel_id=1, source_target_pairs={{0,1},{1,0},{2,3},{3,2},{4,5},{5,4},{6,7},{7,6},{8,9},{9,8},{10,11... | collective-permute-start | bytes 589832 | tf_op jit(solution)/shard_map/ppermute | solution.py:331
  69.6 7.4 %copy-start.2 = (f32[2,2,16,768]{3,2,1,0:T(8,128)}, f32[2,2,16,768]{3,2,1,0:T(8,128)S(1)}, u32[]{:S(2)}) copy-start(f32[2,2,16,768]{3,2,1,0:T(8,128)S(1)} %collective-permute-done.1.f1) | copy-start | bytes 589828
  91.8 38.0 %all-to-all-start.4 = ((bf16[32,272,128]{2,1,0:T(8,128)(2,1)}), bf16[32,272,128]{2,1,0:T(8,128)(2,1)}, u32[]{:S(2)}, u32[]{:S(2)}) async-start(bf16[32,272,128]{2,1,0:T(8,128)(2,1)} %spectral.3), calls=%async_computation.4 | async-start | bytes 4456448 | tf_op jit(solution)/shard_map/all_to_all | solution.py:335
  111.2 25.0 %copy-start.3 = (f32[90]{0:T(128)S(1)}, f32[90]{0:T(128)}, u32[]{:S(2)}) copy-start(f32[90]{0:T(128)} %param.10) | copy-start | bytes 1084
  129.8 24.2 %all-to-all-start.2 = ((bf16[32,136,128]{2,1,0:T(8,128)(2,1)}), bf16[32,136,128]{2,1,0:T(8,128)(2,1)}, u32[]{:S(2)}, u32[]{:S(2)}) async-start(bf16[32,136,128]{2,1,0:T(8,128)(2,1)} %spectral.2), calls=%async_computation.2 | async-start | bytes 2228224 | tf_op jit(solution)/shard_map/all_to_all | solution.py:336

commit v3 on v2

--- a/solution.py
+++ b/solution.py
@@ -38,6 +38,14 @@
     return (SLOTS * count * HALF + 7) // 8 * 8
 
 
+def low_lanes(order_ref):
+    lane = lax.broadcasted_iota(jnp.int32, (1, LANES), 1)
+    low = jnp.zeros((1, LANES), jnp.int32)
+    for j in range(PAIRS):
+        low = jnp.where(lane == j, order_ref[j % DEST * SLOTS + j // DEST], low)
+    return low
+
+
 def fill_table(low, table, coarse_cos, coarse_sin):
     orders = jnp.concatenate([low, M - 1 - low], axis=1)
     unit = 2.0 * math.pi / NLON
@@ -64,27 +72,29 @@
         table[rows, 3 * LANES :] = odd[:, LANES:]
 
 
-def first_forward_kernel(low_ref, x_ref, out_ref, table_ref, product, packed, coarse_cos, coarse_sin):
+def first_forward_kernel(order_ref, x_ref, out_ref, table_ref, product, packed, factor, coarse_cos, coarse_sin):
     @pl.when((pl.program_id(0) == 0) & (pl.program_id(1) == 0))
     def _():
-        fill_table(low_ref[...], table_ref, coarse_cos, coarse_sin)
+        low = low_lanes(order_ref)
+        fill_table(low, table_ref, coarse_cos, coarse_sin)
+        factor[...] = jnp.where(low == 0, 1.0, 2.0).astype(jnp.float32)
         packed[...] = jnp.zeros_like(packed)
 
-    transform(low_ref, x_ref, table_ref, out_ref, product, packed)
-
-
-def later_forward_kernel(low_ref, x_ref, table_ref, out_ref, product, packed):
+    transform(x_ref, table_ref, out_ref, product, packed, factor)
+
+
+def later_forward_kernel(order_ref, x_ref, table_ref, out_ref, product, packed, factor):
     @pl.when((pl.program_id(0) == 0) & (pl.program_id(1) == 0))
     def _():
+        factor[...] = jnp.where(low_lanes(order_ref) == 0, 1.0, 2.0).astype(jnp.float32)
         packed[...] = jnp.zeros_like(packed)
 
-    transform(low_ref, x_ref, table_ref, out_ref, product, packed)
-
-
-def transform(low_ref, x_ref, table_ref, out_ref, product, packed):
+    transform(x_ref, table_ref, out_ref, product, packed, factor)
+
+
+def transform(x_ref, table_ref, out_ref, product, packed, factor):
     sample, count = pl.program_id(0), pl.num_programs(0)
     rows_each = out_ref.shape[1]
-    factor = jnp.where(low_ref[...] == 0, 1.0, 2.0).astype(jnp.float32)
 
     block = x_ref[0].reshape(HALF * CH, NLON)
     rows = pl.ds(pl.multiple_of(pl.program_id(1) * HALF * CH, CH), HALF * CH)
@@ -98,7 +108,7 @@
             for t in range(CHUNK):
                 pieces = []
                 for q in range(4):
-                    scale = factor if q < 2 else 2.0
+                    scale = factor[...] if q < 2 else 2.0
                     for half in range(2):
                         rows = pl.ds(pl.multiple_of((half * HALF + first + t) * CH, CH), CH)
                         pieces.append(product[rows, q * LANES : (q + 1) * LANES] * scale)
@@ -113,16 +123,17 @@
             out_ref[device] = packed[device * rows_each : (device + 1) * rows_each, :].astype(out_ref.dtype)
 
 
-def forward(low, grad, start, count, table=None):
+def forward(pair_order, grad, start, count, table=None):
     whole = pl.BlockSpec((NLON, COLS), lambda s, half: (0, 0))
     in_specs = [
-        pl.BlockSpec((1, LANES), lambda s, half: (0, 0)),
+        pl.BlockSpec(memory_space=pltpu.SMEM),
         pl.BlockSpec((1, HALF, CH, NLON), lambda s, half: (s + start, half, 0, 0)),
     ]
     shape = (DEST, packed_rows(count), LANES)
     out_specs = [pl.BlockSpec(shape, lambda s, half: (0, 0, 0))]
     out_shape = [jax.ShapeDtypeStruct(shape, jnp.bfloat16)]
     scratch = [pltpu.VMEM((LAT * CH, COLS), jnp.float32), pltpu.VMEM((DEST * packed_rows(count), LANES), jnp.float32)]
+    scratch.append(pltpu.VMEM((1, LANES), jnp.float32))
     if table is None:
         out_specs.append(whole)
         out_shape.append(jax.ShapeDtypeStruct((NLON, COLS), jnp.bfloat16))
@@ -139,7 +150,7 @@
         compiler_params=pltpu.CompilerParams(vmem_limit_bytes=VMEM),
         cost_estimate=pl.CostEstimate(flops=4 * count * 1440 * NLON * COLS, bytes_accessed=count * 6_000_000, transcendentals=0),
         name="forward",
-    )(low, grad, *([] if table is None else [table]))
+    )(pair_order, grad, *([] if table is None else [table]))
 
 
 def spectral_kernel(count, low_ref, place_ref, f0, f1, x_ref, t0, t1, t2, t3, out_ref, legendre, columns, split, synthesis, gains, wide, sems):
@@ -308,6 +319,10 @@
     )(scale, table, received, *([] if done is None else [done]))
 
 
+def padded_filters(filter_re, filter_im):
+    return jnp.pad(jnp.stack([filter_re, filter_im]), ((0, 0), (0, 0), (0, ROWS - M)))
+
+
 def body(grad_out, legendre, filter_re, filter_im, quad_weight, pair_order):
     group = lax.axis_index("x_hi") * 2 + lax.axis_index("core")
     z = lax.axis_index("z")
@@ -315,19 +330,17 @@
 
     own = lax.all_to_all(legendre.reshape(GROUPS, SLOTS, HALF, ROWS), ("x_hi", "core"), 0, 0)
 
-    filters = jnp.pad(jnp.stack([filter_re, filter_im]), ((0, 0), (0, 0), (0, ROWS - M)))
-    far = lax.ppermute(filters, "x_hi", [(0, 1), (1, 0)])
-
-    low_lanes = jnp.pad(pair_order.reshape(DEST, SLOTS).T.reshape(1, PAIRS), ((0, 0), (0, LANES - PAIRS)))
+    far = lax.ppermute(padded_filters(filter_re, filter_im), "x_hi", [(0, 1), (1, 0)])
+
     grad = jnp.transpose(grad_out, (0, 2, 1, 3))
-    packed, table = forward(low_lanes, grad, 0, EARLY)
-    packed, own, far = lax.optimization_barrier((packed, own, far))
+    packed, table = forward(pair_order, grad, 0, EARLY)
+    packed, own, far, filter_re, filter_im = lax.optimization_barrier((packed, own, far, filter_re, filter_im))
     early = lax.all_to_all(packed, SLOT_AXES, 0, 0)
     own = jnp.pad(own, ((0, 0), (0, 0), (0, HP - HALF), (0, 0)))
     tables = [own] + [lax.ppermute(own, "z", [(i, (i + shift) % 4) for i in range(4)]) for shift in range(1, 4)]
-    (packed,) = forward(low_lanes, grad, EARLY, SAMPLES - EARLY, table)
+    (packed,) = forward(pair_order, grad, EARLY, SAMPLES - EARLY, table)
     late = lax.all_to_all(packed, SLOT_AXES, 0, 0)
-    near = jnp.stack([filters, far])
+    near = jnp.stack([padded_filters(filter_re, filter_im), far])
     filters = [near, lax.ppermute(near, "core", [(0, 1), (1, 0)])]
 
     low = lax.dynamic_slice_in_dim(pair_order, mine * SLOTS, SLOTS)

time: 162 us -> 160 us (0.988)
  transfers between devices with their start and end apart: 10 -> 10, of which waited for: 5 -> 5; matrix products, arithmetic and copies ran while one was open for 4% -> 3% of each run, Pallas kernels for 36% -> 37%
where the time goes in v3:
time: 160 us; the launch traced here: 159 us
  Pallas kernels  65.2 us (41%)
  waiting for transfers between devices  49.2 us (31%)
  starting transfers between devices  39.5 us (25%)
  local copies, waits for them, and re-layouts  2.49 us (2%)
  other arithmetic  2.36 us (1%)
    pallas_call x2, Pallas kernels, spectral(): pl.pallas_call(functools.partial(spectral_kernel, count), grid=(SLOTS,),...  26.4 us
    pallas_call x2, Pallas kernels, forward(): pl.pallas_call(first_forward_kernel if table is None else later_forward_k...  20.6 us
    all_to_all x1, waiting for transfers between devices, body(): lax.all_to_all(spectral(low, place, filters, early, tables, EARLY), SLOT_...  18.6 us
    pallas_call x2, Pallas kernels, inverse(): pl.pallas_call(inverse_kernel if done is None else later_inverse_kernel,...  18.2 us
    all_to_all x1, waiting for transfers between devices, body(): early = lax.all_to_all(packed, SLOT_AXES, 0, 0)  17.6 us
    all_to_all x1, starting transfers between devices, body(): lax.all_to_all(spectral(low, place, filters, early, tables, EARLY), SLOT_...  7.86 us
    ppermute x3, waiting for transfers between devices, body(): lax.ppermute(own, 'z', [(i, (i + shift) % 4) for i in range(4)])  7.4 us
    all_to_all x1, starting transfers between devices, body(): lax.all_to_all(spectral(low, place, filters, late, tables, SAMPLES - EARL...  6.32 us
  transfers between devices with their start and end apart: 10, of which 5 were waited for; matrix products, arithmetic and copies ran while one was open for 3% of the time, Pallas kernels for 37%

profile of v3, /device:TPU:1, one launch (start us, length us, event | category | flops | bytes accessed | tf_op | source)
XLA Modules:
  0.0 158.9 jit_solution(4679759719154709595)
XLA Ops:
  0.0 5.8 %all-to-all-start = ((bf16[4,3,45,768]{3,2,1,0:T(8,128)(2,1)}), bf16[4,3,45,768]{3,2,1,0:T(8,128)(2,1)S(1)}, u32[]{:S(2)}, u32[]{:S(2)}) async-start(bf16[4,3,45,768]{3,2,1,0:T(8,128)(2,1)} %bitcast.14), calls=%async_computation | async-start | bytes 1769472 | tf_op jit(solution)/shard_map/all_to_all | solution.py:331
  5.8 0.8 fusion.3
  6.6 3.0 %collective-permute-start = (f32[2,16,768]{2,1,0:T(8,128)S(1)}, f32[2,16,768]{2,1,0:T(8,128)}, u32[]{:S(2)}, u32[]{:S(2)}) collective-permute-start(f32[2,16,768]{2,1,0:T(8,128)S(1)} %fusion.3), channel_id=1, source_target_pairs={{0,8},{8,0},{1,9},{9,1},{2,10},{10,2},{3,11},{11,3},{4,12},{12,4},... | collective-permute-start | bytes 294920 | tf_op jit(solution)/shard_map/ppermute | solution.py:333
  9.6 13.4 %forward.2 = (bf16[32,272,128]{2,1,0:T(8,128)(2,1)}, bf16[1440,512]{1,0:T(8,128)(2,1)}) custom-call(s32[96]{0:T(128)} %order_ref.3, bf16[3,90,16,1440]{3,2,1,0:T(8,128)(2,1)} %bitcast.12), custom_call_target="tpu_custom_call" | custom-call | flops 8493465600 | bytes 12000000 | tf_op jit(solution)/shard_map/forward/pallas_call | solution.py:143
  23.0 5.4 %all-to-all-start.3 = ((bf16[32,272,128]{2,1,0:T(8,128)(2,1)}), bf16[32,272,128]{2,1,0:T(8,128)(2,1)}, u32[]{:S(2)}, u32[]{:S(2)}) async-start(bf16[32,272,128]{2,1,0:T(8,128)(2,1)} %get-tuple-element.18), calls=%async_computation.3 | async-start | bytes 4456448 | tf_op jit(solution)/shard_map/all_to_all | solution.py:338
  28.5 1.0 pad.13.t0
  29.5 3.8 %collective-permute-start.4 = (bf16[4,3,48,768]{3,2,1,0:T(8,128)(2,1)}, bf16[4,3,48,768]{3,2,1,0:T(8,128)(2,1)}, u32[]{:S(2)}, u32[]{:S(2)}) collective-permute-start(bf16[4,3,48,768]{3,2,1,0:T(8,128)(2,1)} %pad.13.t0), channel_id=1, source_target_pairs={{0,6},{2,0},{4,2},{6,4},{1,7},{3,1},{5,3},{7,5},{8,14},{10,8},{12,... | collective-permute-start | bytes 2654216 | tf_op jit(solution)/shard_map/ppermute | solution.py:340
  33.2 0.7 collective-permute-start.2
  33.9 7.2 %forward.3 = bf16[32,136,128]{2,1,0:T(8,128)(2,1)} custom-call(s32[96]{0:T(128)} %order_ref.3, bf16[3,90,16,1440]{3,2,1,0:T(8,128)(2,1)} %bitcast.13, bf16[1440,512]{1,0:T(8,128)(2,1)} %get-tuple-element.12.table_ref), custom_call_target="tpu_custom_call" | custom-call | flops 4246732800 | bytes 6000000 | tf_op jit(solution)/shard_map/forward/pallas_call | solution.py:143
  41.1 17.6 %all-to-all-done.3.x_ref = bf16[32,272,128]{2,1,0:T(8,128)(2,1)} async-done(((bf16[32,272,128]{2,1,0:T(8,128)(2,1)}), bf16[32,272,128]{2,1,0:T(8,128)(2,1)}, u32[]{:S(2)}, u32[]{:S(2)}) %all-to-all-start.3) | async-done | bytes 2228256 | tf_op jit(solution)/shard_map/all_to_all | solution.py:338
  58.6 6.3 %all-to-all-start.1 = ((bf16[32,136,128]{2,1,0:T(8,128)(2,1)}), bf16[32,136,128]{2,1,0:T(8,128)(2,1)}, u32[]{:S(2)}, u32[]{:S(2)}) async-start(bf16[32,136,128]{2,1,0:T(8,128)(2,1)} %forward.3), calls=%async_computation.1 | async-start | bytes 2228224 | tf_op jit(solution)/shard_map/all_to_all | solution.py:342
  65.0 0.9 pad_maximum_fusion.f0
  66.3 0.6 dynamic_slice.3.low_ref
  67.6 3.7 %collective-permute-done.4.t3 = bf16[4,3,48,768]{3,2,1,0:T(8,128)(2,1)} collective-permute-done((bf16[4,3,48,768]{3,2,1,0:T(8,128)(2,1)}, bf16[4,3,48,768]{3,2,1,0:T(8,128)(2,1)}, u32[]{:S(2)}, u32[]{:S(2)}) %collective-permute-start.4) | collective-permute-done | bytes 884768 | tf_op jit(solution)/shard_map/ppermute | solution.py:340
  71.2 3.7 %collective-permute-done.2.t1 = bf16[4,3,48,768]{3,2,1,0:T(8,128)(2,1)} collective-permute-done((bf16[4,3,48,768]{3,2,1,0:T(8,128)(2,1)}, bf16[4,3,48,768]{3,2,1,0:T(8,128)(2,1)}, u32[]{:S(2)}, u32[]{:S(2)}) %collective-permute-start.2) | collective-permute-done | bytes 884768 | tf_op jit(solution)/shard_map/ppermute | solution.py:340
  75.0 14.8 %spectral.3 = bf16[32,272,128]{2,1,0:T(8,128)(2,1)} custom-call(s32[3]{0:T(128)} %dynamic_slice.3.low_ref, s32[2]{0:T(128)} %pad_add_fusion.place_ref, f32[2,2,16,768]{3,2,1,0:T(8,128)} %copy-done, f32[2,2,16,768]{3,2,1,0:T(8,128)} %copy-done.4, bf16[32,272,128]{2,1,0:T(8,128)(2,1)} %all-to-all-done.3.x_ref, bf16[4,3,48,768]{3,2,1,0:T(8,128)(2,1)} %pad.13.t0, ...), custom_call_target="tpu_custom_call" | custom-call | flops 3623878656 | bytes 12000000 | tf_op jit(solution)/shard_map/spectral/pallas_call | solution.py:240
  89.8 7.9 %all-to-all-start.4 = ((bf16[32,272,128]{2,1,0:T(8,128)(2,1)}), bf16[32,272,128]{2,1,0:T(8,128)(2,1)}, u32[]{:S(2)}, u32[]{:S(2)}) async-start(bf16[32,272,128]{2,1,0:T(8,128)(2,1)} %spectral.3), calls=%async_computation.4 | async-start | bytes 4456448 | tf_op jit(solution)/shard_map/all_to_all | solution.py:348
  97.7 11.5 %spectral.2 = bf16[32,136,128]{2,1,0:T(8,128)(2,1)} custom-call(s32[3]{0:T(128)} %dynamic_slice.3.low_ref, s32[2]{0:T(128)} %pad_add_fusion.place_ref, f32[2,2,16,768]{3,2,1,0:T(8,128)} %copy-done, f32[2,2,16,768]{3,2,1,0:T(8,128)} %copy-done.4, bf16[32,136,128]{2,1,0:T(8,128)(2,1)} %all-to-all-done.1.x_ref, bf16[4,3,48,768]{3,2,1,0:T(8,128)(2,1)} %pad.13.t0, ...), custom_call_target="tpu_custom_call" | custom-call | flops 1811939328 | bytes 12000000 | tf_op jit(solution)/shard_map/spectral/pallas_call | solution.py:240
  109.3 18.6 %all-to-all-done.4.x_ref = bf16[32,272,128]{2,1,0:T(8,128)(2,1)} async-done(((bf16[32,272,128]{2,1,0:T(8,128)(2,1)}), bf16[32,272,128]{2,1,0:T(8,128)(2,1)}, u32[]{:S(2)}, u32[]{:S(2)}) %all-to-all-start.4) | async-done | bytes 2228256 | tf_op jit(solution)/shard_map/all_to_all | solution.py:348
  127.9 6.3 %all-to-all-start.2 = ((bf16[32,136,128]{2,1,0:T(8,128)(2,1)}), bf16[32,136,128]{2,1,0:T(8,128)(2,1)}, u32[]{:S(2)}, u32[]{:S(2)}) async-start(bf16[32,136,128]{2,1,0:T(8,128)(2,1)} %spectral.2), calls=%async_computation.2 | async-start | bytes 2228224 | tf_op jit(solution)/shard_map/all_to_all | solution.py:349
  134.2 0.8 broadcast_in_dim.2.scale_ref
  135.1 11.4 %inverse.2.done_ref = bf16[3,90,16,1440]{3,2,1,0:T(8,128)(2,1)} custom-call(f32[90,1,512]{2,1,0:T(1,128)} %broadcast_in_dim.2.scale_ref, bf16[1440,512]{1,0:T(8,128)(2,1)} %get-tuple-element.12.table_ref, bf16[32,272,128]{2,1,0:T(8,128)(2,1)} %all-to-all-done.4.x_ref), custom_call_target="tpu_custom_call" | custom-call | flops 8493465600 | bytes 12000000 | tf_op jit(solution)/shard_map/inverse/pallas_call | solution.py:305
  146.4 5.6 %all-to-all-done.2.x_ref = bf16[32,136,128]{2,1,0:T(8,128)(2,1)} async-done(((bf16[32,136,128]{2,1,0:T(8,128)(2,1)}), bf16[32,136,128]{2,1,0:T(8,128)(2,1)}, u32[]{:S(2)}, u32[]{:S(2)}) %all-to-all-start.2) | async-done | bytes 1114144 | tf_op jit(solution)/shard_map/all_to_all | solution.py:349
  152.0 6.8 %inverse.3 = bf16[3,90,16,1440]{3,2,1,0:T(8,128)(2,1)} custom-call(f32[90,1,512]{2,1,0:T(1,128)} %broadcast_in_dim.2.scale_ref, bf16[1440,512]{1,0:T(8,128)(2,1)} %get-tuple-element.12.table_ref, bf16[32,136,128]{2,1,0:T(8,128)(2,1)} %all-to-all-done.2.x_ref, bf16[3,90,16,1440]{3,2,1,0:T(8,128)(2,1)} %inverse.2.done_ref), custom_call_target="tpu_custom_call", output_to_operand_aliasing={{}: (3, {})} | custom-call | flops 4246732800 | bytes 6000000 | tf_op jit(solution)/shard_map/inverse/pallas_call | solution.py:305
  (22 shorter events, 1.0 us)
Async XLA Ops:
  0.0 23.0 %all-to-all-start = ((bf16[4,3,45,768]{3,2,1,0:T(8,128)(2,1)}), bf16[4,3,45,768]{3,2,1,0:T(8,128)(2,1)S(1)}, u32[]{:S(2)}, u32[]{:S(2)}) async-start(bf16[4,3,45,768]{3,2,1,0:T(8,128)(2,1)} %bitcast.14), calls=%async_computation | async-start | bytes 1769472 | tf_op jit(solution)/shard_map/all_to_all | solution.py:331
  6.6 16.4 %collective-permute-start = (f32[2,16,768]{2,1,0:T(8,128)S(1)}, f32[2,16,768]{2,1,0:T(8,128)}, u32[]{:S(2)}, u32[]{:S(2)}) collective-permute-start(f32[2,16,768]{2,1,0:T(8,128)S(1)} %fusion.3), channel_id=1, source_target_pairs={{0,8},{8,0},{1,9},{9,1},{2,10},{10,2},{3,11},{11,3},{4,12},{12,4},... | collective-permute-start | bytes 294920 | tf_op jit(solution)/shard_map/ppermute | solution.py:333
  23.0 35.6 %all-to-all-start.3 = ((bf16[32,272,128]{2,1,0:T(8,128)(2,1)}), bf16[32,272,128]{2,1,0:T(8,128)(2,1)}, u32[]{:S(2)}, u32[]{:S(2)}) async-start(bf16[32,272,128]{2,1,0:T(8,128)(2,1)} %get-tuple-element.18), calls=%async_computation.3 | async-start | bytes 4456448 | tf_op jit(solution)/shard_map/all_to_all | solution.py:338
  29.5 41.8 %collective-permute-start.4 = (bf16[4,3,48,768]{3,2,1,0:T(8,128)(2,1)}, bf16[4,3,48,768]{3,2,1,0:T(8,128)(2,1)}, u32[]{:S(2)}, u32[]{:S(2)}) collective-permute-start(bf16[4,3,48,768]{3,2,1,0:T(8,128)(2,1)} %pad.13.t0), channel_id=1, source_target_pairs={{0,6},{2,0},{4,2},{6,4},{1,7},{3,1},{5,3},{7,5},{8,14},{10,8},{12,... | collective-permute-start | bytes 2654216 | tf_op jit(solution)/shard_map/ppermute | solution.py:340
  33.2 38.0 %collective-permute-start.3 = (bf16[4,3,48,768]{3,2,1,0:T(8,128)(2,1)}, bf16[4,3,48,768]{3,2,1,0:T(8,128)(2,1)}, u32[]{:S(2)}, u32[]{:S(2)}) collective-permute-start(bf16[4,3,48,768]{3,2,1,0:T(8,128)(2,1)} %pad.13.t0), channel_id=1, source_target_pairs={{0,4},{2,6},{4,0},{6,2},{1,5},{3,7},{5,1},{7,3},{8,12},{10,14},{12... | collective-permute-start | bytes 2654216 | tf_op jit(solution)/shard_map/ppermute | solution.py:340
  33.2 41.8 %collective-permute-start.2 = (bf16[4,3,48,768]{3,2,1,0:T(8,128)(2,1)}, bf16[4,3,48,768]{3,2,1,0:T(8,128)(2,1)}, u32[]{:S(2)}, u32[]{:S(2)}) collective-permute-start(bf16[4,3,48,768]{3,2,1,0:T(8,128)(2,1)} %pad.13.t0), channel_id=1, source_target_pairs={{0,2},{2,4},{4,6},{6,0},{1,3},{3,5},{5,7},{7,1},{8,10},{10,12},{12... | collective-permute-start | bytes 2654216 | tf_op jit(solution)/shard_map/ppermute | solution.py:340
  41.1 23.9 %copy-start.1 = (f32[16,720]{1,0:T(8,128)S(1)}, f32[16,720]{1,0:T(8,128)}, u32[]{:S(2)}) copy-start(f32[16,720]{1,0:T(8,128)} %param.9) | copy-start | bytes 138244
  41.1 23.9 %copy-start.2 = (f32[16,720]{1,0:T(8,128)S(1)}, f32[16,720]{1,0:T(8,128)}, u32[]{:S(2)}) copy-start(f32[16,720]{1,0:T(8,128)} %param.8) | copy-start | bytes 138244
  41.1 25.2 %copy-start.3 = (s32[96]{0:T(128)S(1)}, s32[96]{0:T(128)}, u32[]{:S(2)}) copy-start(s32[96]{0:T(128)} %order_ref.3) | copy-start | bytes 1156
  58.6 31.2 %all-to-all-start.1 = ((bf16[32,136,128]{2,1,0:T(8,128)(2,1)}), bf16[32,136,128]{2,1,0:T(8,128)(2,1)}, u32[]{:S(2)}, u32[]{:S(2)}) async-start(bf16[32,136,128]{2,1,0:T(8,128)(2,1)} %forward.3), calls=%async_computation.1 | async-start | bytes 2228224 | tf_op jit(solution)/shard_map/all_to_all | solution.py:342
  65.9 9.1 %copy-start = (f32[2,2,16,768]{3,2,1,0:T(8,128)}, f32[2,2,16,768]{3,2,1,0:T(8,128)S(1)}, u32[]{:S(2)}) copy-start(f32[2,2,16,768]{3,2,1,0:T(8,128)S(1)} %pad_maximum_fusion.f0) | copy-start | bytes 589828
  65.9 1.6 %collective-permute-start.1 = (f32[2,2,16,768]{3,2,1,0:T(8,128)S(1)}, f32[2,2,16,768]{3,2,1,0:T(8,128)S(1)}, u32[]{:S(2)}, u32[]{:S(2)}) collective-permute-start(f32[2,2,16,768]{3,2,1,0:T(8,128)S(1)} %pad_maximum_fusion.f0), channel_id=1, source_target_pairs={{0,1},{1,0},{2,3},{3,2},{4,5},{5,4},{6,7},{7,6},{8,9},{9,8},{10,11... | collective-permute-start | bytes 589832 | tf_op jit(solution)/shard_map/ppermute | solution.py:344
  67.6 7.4 %copy-start.4 = (f32[2,2,16,768]{3,2,1,0:T(8,128)}, f32[2,2,16,768]{3,2,1,0:T(8,128)S(1)}, u32[]{:S(2)}) copy-start(f32[2,2,16,768]{3,2,1,0:T(8,128)S(1)} %collective-permute-done.1.f1) | copy-start | bytes 589828
  89.8 38.0 %all-to-all-start.4 = ((bf16[32,272,128]{2,1,0:T(8,128)(2,1)}), bf16[32,272,128]{2,1,0:T(8,128)(2,1)}, u32[]{:S(2)}, u32[]{:S(2)}) async-start(bf16[32,272,128]{2,1,0:T(8,128)(2,1)} %spectral.3), calls=%async_computation.4 | async-start | bytes 4456448 | tf_op jit(solution)/shard_map/all_to_all | solution.py:348
  109.2 25.0 %copy-start.5 = (f32[90]{0:T(128)S(1)}, f32[90]{0:T(128)}, u32[]{:S(2)}) copy-start(f32[90]{0:T(128)} %param.10) | copy-start | bytes 1084
  127.9 24.1 %all-to-all-start.2 = ((bf16[32,136,128]{2,1,0:T(8,128)(2,1)}), bf16[32,136,128]{2,1,0:T(8,128)(2,1)}, u32[]{:S(2)}, u32[]{:S(2)}) async-start(bf16[32,136,128]{2,1,0:T(8,128)(2,1)} %spectral.2), calls=%async_computation.2 | async-start | bytes 2228224 | tf_op jit(solution)/shard_map/all_to_all | solution.py:349

commit v4 on v3

--- a/solution.py
+++ b/solution.py
@@ -153,11 +153,64 @@
     )(pair_order, grad, *([] if table is None else [table]))
 
 
-def spectral_kernel(count, low_ref, place_ref, f0, f1, x_ref, t0, t1, t2, t3, out_ref, legendre, columns, split, synthesis, gains, wide, sems):
+def place(order, pair, offset, piece, rows_each):
+    return (order * GROUPS + pair * 2 + offset) * rows_each + piece * HALF
+
+
+def column_tiles(count):
+    return [
+        (sample, pair, slice((sample * 2 + pair) * LANES, (sample * 2 + pair + 1) * LANES))
+        for sample in range(count)
+        for pair in range(2)
+    ]
+
+
+def shuffle(a, b):
+    lane = lax.broadcasted_iota(jnp.int32, (HP, LANES), 1)
+    former_half = lax.rem(lax.div(lane, CH), 2) == 0
+    return jnp.where(former_half, a, pltpu.roll(b, CH, 1)), jnp.where(former_half, pltpu.roll(a, LANES - CH, 1), b)
+
+
+def columns_kernel(count, x_ref, out_ref, wide):
+    slot = pl.program_id(0)
+    rows_each = x_ref.shape[1]
+
+    @pl.when(slot == 0)
+    def _():
+        for device in range(DEST):
+            wide[device * rows_each : (device + 1) * rows_each, :] = x_ref[device].astype(jnp.float32)
+        wide[DEST * rows_each :, :] = jnp.zeros((EXTRA, LANES), jnp.float32)
+
+    @pl.loop(0, 8)
+    def _(order):
+        for sample, pair, lanes in column_tiles(count):
+            a, b = (wide[pl.ds(place(order, pair, offset, slot * count + sample, rows_each), HP), :] for offset in range(2))
+            for half, value in enumerate(shuffle(a, b)):
+                rows = pl.ds(pl.multiple_of((order * 2 + half) * HP, HP), HP)
+                out_ref[0, rows, lanes] = value.astype(out_ref.dtype)
+
+
+def columns_of(received, count):
+    width = count * 2 * LANES
+    return pl.pallas_call(
+        functools.partial(columns_kernel, count),
+        grid=(SLOTS,),
+        in_specs=[pl.BlockSpec(received.shape, lambda slot: (0, 0, 0))],
+        out_specs=pl.BlockSpec((1, 16 * HP, width), lambda slot: (slot, 0, 0)),
+        out_shape=jax.ShapeDtypeStruct((SLOTS, 16 * HP, width), jnp.bfloat16),
+        scratch_shapes=[pltpu.VMEM((DEST * packed_rows(count) + EXTRA, LANES), jnp.float32)],
+        compiler_params=pltpu.CompilerParams(vmem_limit_bytes=VMEM),
+        cost_estimate=pl.CostEstimate(flops=10_000_000, bytes_accessed=5_000_000, transcendentals=0),
+        name="columns",
+    )(received)
+
+
+def spectral_kernel(count, low_ref, place_ref, f0, f1, columns, t0, t1, t2, t3, out_ref, legendre, split, synthesis, gains, wide, sems):
     slot = pl.program_id(0)
     group, z = place_ref[0], place_ref[1]
 
-    rows_each = x_ref.shape[1]
+    rows_each = out_ref.shape[1]
+    tiles = column_tiles(count)
 
     def table_copies(which):
         copies = []
@@ -172,9 +225,9 @@
         for which in range(SLOTS):
             for copy in table_copies(which):
                 copy.start()
-        for device in range(DEST):
-            wide[device * rows_each : (device + 1) * rows_each, :] = x_ref[device].astype(jnp.float32)
-        wide[DEST * rows_each :, :] = jnp.zeros((EXTRA, LANES), jnp.float32)
+        used = SLOTS * count * HALF
+        for device in range(DEST):
+            wide[device * rows_each + used : (device + 1) * rows_each, :] = jnp.zeros((rows_each - used, LANES), jnp.float32)
 
     low = low_ref[slot]
     below = lax.broadcasted_iota(jnp.int32, (1, ROWS), 1) < M - low
@@ -184,29 +237,10 @@
             whole = (f1 if k % 2 else f0)[k // 2, part]
             gains[part, rows, :] = jnp.where(below, pltpu.roll(whole, ROWS - low, 1), pltpu.roll(whole, 1, 1))
 
-    lane = lax.broadcasted_iota(jnp.int32, (HP, LANES), 1)
-    former_half = lax.rem(lax.div(lane, CH), 2) == 0
-
-    def shuffle(a, b):
-        return jnp.where(former_half, a, pltpu.roll(b, CH, 1)), jnp.where(former_half, pltpu.roll(a, LANES - CH, 1), b)
-
-    tiles = [(sample, pair, slice((sample * 2 + pair) * LANES, (sample * 2 + pair + 1) * LANES)) for sample in range(count) for pair in range(2)]
-
-    def place(order, pair, offset, sample):
-        return (order * GROUPS + pair * 2 + offset) * rows_each + (slot * count + sample) * HALF
-
-    @pl.loop(0, 8)
-    def _(order):
-        for sample, pair, lanes in tiles:
-            a, b = (wide[pl.ds(place(order, pair, offset, sample), HP), :] for offset in range(2))
-            for half, value in enumerate(shuffle(a, b)):
-                rows = pl.ds(pl.multiple_of((order * 2 + half) * HP, HP), HP)
-                columns[rows, lanes] = value.astype(columns.dtype)
-
     for copy in table_copies(slot):
         copy.wait()
     table = legendre[slot].reshape(16 * HP, ROWS)
-    spectrum = lax.dot_general(columns[...], table, TN, preferred_element_type=jnp.float32)
+    spectrum = lax.dot_general(columns[0], table, TN, preferred_element_type=jnp.float32)
     for sample, pair, lanes in tiles:
         a0, a1, a2, a3 = (spectrum[lanes.start + q * 32 : lanes.start + (q + 1) * 32] for q in range(4))
         former, latter = jnp.where(below, a0, a2), jnp.where(below, a1, a3)
@@ -223,7 +257,7 @@
         for sample, pair, lanes in tiles:
             halves = [synthesis[pl.ds(pl.multiple_of((order * 2 + half) * HP, HP), HP), lanes] for half in range(2)]
             for offset, value in enumerate(shuffle(*halves)):
-                wide[pl.ds(place(order, pair, offset, sample), HALF), :] = value[:HALF]
+                wide[pl.ds(place(order, pair, offset, slot * count + sample, rows_each), HALF), :] = value[:HALF]
 
     @pl.when(slot == SLOTS - 1)
     def _():
@@ -231,21 +265,20 @@
             out_ref[device] = wide[device * rows_each : (device + 1) * rows_each, :].astype(out_ref.dtype)
 
 
-def spectral(low, place, filters, received, tables, count):
+def spectral(low, where, filters, received, tables, count):
     width = count * 2 * LANES
-    block = pl.BlockSpec(received.shape, lambda slot: (0, 0, 0))
+    shape = (DEST, packed_rows(count), LANES)
     smem = pl.BlockSpec(memory_space=pltpu.SMEM)
     hbm = pl.BlockSpec(memory_space=pl.ANY)
     gain = pl.BlockSpec((2, 2, CH, ROWS), lambda slot: (0, 0, 0, 0))
     return pl.pallas_call(
         functools.partial(spectral_kernel, count),
         grid=(SLOTS,),
-        in_specs=[smem, smem] + [gain] * 2 + [block] + [hbm] * 4,
-        out_specs=block,
-        out_shape=jax.ShapeDtypeStruct(received.shape, jnp.bfloat16),
+        in_specs=[smem, smem] + [gain] * 2 + [pl.BlockSpec((1, 16 * HP, width), lambda slot: (slot, 0, 0))] + [hbm] * 4,
+        out_specs=pl.BlockSpec(shape, lambda slot: (0, 0, 0)),
+        out_shape=jax.ShapeDtypeStruct(shape, jnp.bfloat16),
         scratch_shapes=[
             pltpu.VMEM((SLOTS, 16, HP, ROWS), jnp.bfloat16),
-            pltpu.VMEM((16 * HP, width), jnp.bfloat16),
             pltpu.VMEM((width, ROWS), jnp.bfloat16),
             pltpu.VMEM((16 * HP, width), jnp.float32),
             pltpu.VMEM((2, GROUPS * CH, ROWS), jnp.float32),
@@ -255,7 +288,7 @@
         compiler_params=pltpu.CompilerParams(vmem_limit_bytes=VMEM),
         cost_estimate=pl.CostEstimate(flops=12 * ROWS * ROWS * width, bytes_accessed=12_000_000, transcendentals=0),
         name="spectral",
-    )(low, place, *filters, received, *tables)
+    )(low, where, *filters, columns_of(received, count), *tables)
 
 
 def later_inverse_kernel(scale_ref, table_ref, x_ref, done_ref, out_ref, packed, left):
@@ -344,9 +377,9 @@
     filters = [near, lax.ppermute(near, "core", [(0, 1), (1, 0)])]
 
     low = lax.dynamic_slice_in_dim(pair_order, mine * SLOTS, SLOTS)
-    place = jnp.stack([group, z])
-    early = lax.all_to_all(spectral(low, place, filters, early, tables, EARLY), SLOT_AXES, 0, 0)
-    late = lax.all_to_all(spectral(low, place, filters, late, tables, SAMPLES - EARLY), SLOT_AXES, 0, 0)
+    where = jnp.stack([group, z])
+    early = lax.all_to_all(spectral(low, where, filters, early, tables, EARLY), SLOT_AXES, 0, 0)
+    late = lax.all_to_all(spectral(low, where, filters, late, tables, SAMPLES - EARLY), SLOT_AXES, 0, 0)
 
     scale = jnp.broadcast_to((quad_weight * (2.0 * math.pi / NLON))[:, None, None], (LAT, 1, 512))
     values = inverse(scale, table, early, 0, EARLY)

time: 160 us -> 158 us (0.988)
  waiting for transfers between devices: 49.2 us -> 41.5 us
  Pallas kernels: 65.2 us -> 70.9 us
    pallas_call x0 -> x2, Pallas kernels: none -> 9.5 us  [columns_of(): pl.pallas_call(functools.partial(columns_kernel, count), grid=(SLOTS,), i...]
    ppermute x3, waiting for transfers between devices: 7.4 us -> 2.36 us  [body(): lax.ppermute(own, 'z', [(i, (i + shift) % 4) for i in range(4)])]
    pallas_call x2, Pallas kernels: 26.4 us -> 22.5 us  [spectral(): pl.pallas_call(functools.partial(spectral_kernel, count), grid=(SLOTS,),...]
    all_to_all x2, waiting for transfers between devices: 24.2 us -> 21.6 us  [the longest x1 16 us: body(): lax.all_to_all(spectral(low, where, filters, early, tables, EARLY), SLOT_...]
  transfers between devices with their start and end apart: 10 -> 10, of which waited for: 5 -> 4; matrix products, arithmetic and copies ran while one was open for 3% -> 3% of each run, Pallas kernels for 37% -> 41%
where the time goes in v4:
time: 158 us; the launch traced here: 157 us
  Pallas kernels  70.9 us (45%)
  waiting for transfers between devices  41.5 us (26%)
  starting transfers between devices  39.5 us (25%)
  local copies, waits for them, and re-layouts  2.51 us (2%)
  other arithmetic  2.31 us (1%)
    pallas_call x2, Pallas kernels, spectral(): pl.pallas_call(functools.partial(spectral_kernel, count), grid=(SLOTS,),...  22.5 us
    pallas_call x2, Pallas kernels, forward(): pl.pallas_call(first_forward_kernel if table is None else later_forward_k...  20.6 us
    pallas_call x2, Pallas kernels, inverse(): pl.pallas_call(inverse_kernel if done is None else later_inverse_kernel,...  18.2 us
    all_to_all x1, waiting for transfers between devices, body(): early = lax.all_to_all(packed, SLOT_AXES, 0, 0)  17.5 us
    all_to_all x1, waiting for transfers between devices, body(): lax.all_to_all(spectral(low, where, filters, early, tables, EARLY), SLOT_...  16 us
    pallas_call x2, Pallas kernels, columns_of(): pl.pallas_call(functools.partial(columns_kernel, count), grid=(SLOTS,), i...  9.5 us
    all_to_all x1, starting transfers between devices, body(): lax.all_to_all(spectral(low, where, filters, early, tables, EARLY), SLOT_...  7.86 us
    all_to_all x1, starting transfers between devices, body(): lax.all_to_all(spectral(low, where, filters, late, tables, SAMPLES - EARL...  6.32 us
  transfers between devices with their start and end apart: 10, of which 4 were waited for; matrix products, arithmetic and copies ran while one was open for 3% of the time, Pallas kernels for 41%

profile of v4, /device:TPU:1, one launch (start us, length us, event | category | flops | bytes accessed | tf_op | source)
XLA Modules:
  0.0 156.8 jit_solution(11727811599439536015)
XLA Ops:
  0.0 5.8 %all-to-all-start = ((bf16[4,3,45,768]{3,2,1,0:T(8,128)(2,1)}), bf16[4,3,45,768]{3,2,1,0:T(8,128)(2,1)S(1)}, u32[]{:S(2)}, u32[]{:S(2)}) async-start(bf16[4,3,45,768]{3,2,1,0:T(8,128)(2,1)} %bitcast.14), calls=%async_computation | async-start | bytes 1769472 | tf_op jit(solution)/shard_map/all_to_all | solution.py:364
  5.8 0.8 fusion.3
  6.6 3.0 %collective-permute-start = (f32[2,16,768]{2,1,0:T(8,128)S(1)}, f32[2,16,768]{2,1,0:T(8,128)}, u32[]{:S(2)}, u32[]{:S(2)}) collective-permute-start(f32[2,16,768]{2,1,0:T(8,128)S(1)} %fusion.3), channel_id=1, source_target_pairs={{0,8},{8,0},{1,9},{9,1},{2,10},{10,2},{3,11},{11,3},{4,12},{12,4},... | collective-permute-start | bytes 294920 | tf_op jit(solution)/shard_map/ppermute | solution.py:366
  9.6 13.5 %forward.2 = (bf16[32,272,128]{2,1,0:T(8,128)(2,1)}, bf16[1440,512]{1,0:T(8,128)(2,1)}) custom-call(s32[96]{0:T(128)} %order_ref.3, bf16[3,90,16,1440]{3,2,1,0:T(8,128)(2,1)} %bitcast.12), custom_call_target="tpu_custom_call" | custom-call | flops 8493465600 | bytes 12000000 | tf_op jit(solution)/shard_map/forward/pallas_call | solution.py:143
  23.1 5.4 %all-to-all-start.3 = ((bf16[32,272,128]{2,1,0:T(8,128)(2,1)}), bf16[32,272,128]{2,1,0:T(8,128)(2,1)}, u32[]{:S(2)}, u32[]{:S(2)}) async-start(bf16[32,272,128]{2,1,0:T(8,128)(2,1)} %get-tuple-element.18), calls=%async_computation.3 | async-start | bytes 4456448 | tf_op jit(solution)/shard_map/all_to_all | solution.py:371
  28.5 1.1 pad.13.t0
  29.6 3.8 %collective-permute-start.4 = (bf16[4,3,48,768]{3,2,1,0:T(8,128)(2,1)}, bf16[4,3,48,768]{3,2,1,0:T(8,128)(2,1)}, u32[]{:S(2)}, u32[]{:S(2)}) collective-permute-start(bf16[4,3,48,768]{3,2,1,0:T(8,128)(2,1)} %pad.13.t0), channel_id=1, source_target_pairs={{0,6},{2,0},{4,2},{6,4},{1,7},{3,1},{5,3},{7,5},{8,14},{10,8},{12,... | collective-permute-start | bytes 2654216 | tf_op jit(solution)/shard_map/ppermute | solution.py:373
  33.3 0.7 collective-permute-start.2
  34.0 7.1 %forward.3 = bf16[32,136,128]{2,1,0:T(8,128)(2,1)} custom-call(s32[96]{0:T(128)} %order_ref.3, bf16[3,90,16,1440]{3,2,1,0:T(8,128)(2,1)} %bitcast.13, bf16[1440,512]{1,0:T(8,128)(2,1)} %get-tuple-element.12.table_ref), custom_call_target="tpu_custom_call" | custom-call | flops 4246732800 | bytes 6000000 | tf_op jit(solution)/shard_map/forward/pallas_call | solution.py:143
  41.2 17.5 %all-to-all-done.3.x_ref = bf16[32,272,128]{2,1,0:T(8,128)(2,1)} async-done(((bf16[32,272,128]{2,1,0:T(8,128)(2,1)}), bf16[32,272,128]{2,1,0:T(8,128)(2,1)}, u32[]{:S(2)}, u32[]{:S(2)}) %all-to-all-start.3) | async-done | bytes 2228256 | tf_op jit(solution)/shard_map/all_to_all | solution.py:371
  58.7 6.3 %all-to-all-start.1 = ((bf16[32,136,128]{2,1,0:T(8,128)(2,1)}), bf16[32,136,128]{2,1,0:T(8,128)(2,1)}, u32[]{:S(2)}, u32[]{:S(2)}) async-start(bf16[32,136,128]{2,1,0:T(8,128)(2,1)} %forward.3), calls=%async_computation.1 | async-start | bytes 2228224 | tf_op jit(solution)/shard_map/all_to_all | solution.py:375
  65.0 0.9 pad_maximum_fusion.f0
  67.5 5.2 %columns.3 = bf16[3,768,512]{2,1,0:T(8,128)(2,1)} custom-call(bf16[32,272,128]{2,1,0:T(8,128)(2,1)} %all-to-all-done.3.x_ref), custom_call_target="tpu_custom_call" | custom-call | flops 10000000 | bytes 5000000 | tf_op jit(solution)/shard_map/columns/pallas_call | solution.py:195
  72.7 2.4 %collective-permute-done.2.t1 = bf16[4,3,48,768]{3,2,1,0:T(8,128)(2,1)} collective-permute-done((bf16[4,3,48,768]{3,2,1,0:T(8,128)(2,1)}, bf16[4,3,48,768]{3,2,1,0:T(8,128)(2,1)}, u32[]{:S(2)}, u32[]{:S(2)}) %collective-permute-start.2) | collective-permute-done | bytes 884768 | tf_op jit(solution)/shard_map/ppermute | solution.py:373
  75.1 12.7 %spectral.3 = bf16[32,272,128]{2,1,0:T(8,128)(2,1)} custom-call(s32[3]{0:T(128)} %dynamic_slice.3.low_ref, s32[2]{0:T(128)} %pad_add_fusion.place_ref, f32[2,2,16,768]{3,2,1,0:T(8,128)} %copy-done, f32[2,2,16,768]{3,2,1,0:T(8,128)} %copy-done.4, bf16[3,768,512]{2,1,0:T(8,128)(2,1)} %columns.3, bf16[4,3,48,768]{3,2,1,0:T(8,128)(2,1)} %pad.13.t0, ...), custom_call_target="tpu_custom_call" | custom-call | flops 3623878656 | bytes 12000000 | tf_op jit(solution)/shard_map/spectral/pallas_call | solution.py:274
  87.8 7.9 %all-to-all-start.4 = ((bf16[32,272,128]{2,1,0:T(8,128)(2,1)}), bf16[32,272,128]{2,1,0:T(8,128)(2,1)}, u32[]{:S(2)}, u32[]{:S(2)}) async-start(bf16[32,272,128]{2,1,0:T(8,128)(2,1)} %spectral.3), calls=%async_computation.4 | async-start | bytes 4456448 | tf_op jit(solution)/shard_map/all_to_all | solution.py:381
  95.6 4.3 %columns.2 = bf16[3,768,256]{2,1,0:T(8,128)(2,1)} custom-call(bf16[32,136,128]{2,1,0:T(8,128)(2,1)} %all-to-all-done.1.x_ref), custom_call_target="tpu_custom_call" | custom-call | flops 10000000 | bytes 5000000 | tf_op jit(solution)/shard_map/columns/pallas_call | solution.py:195
  99.9 9.9 %spectral.2 = bf16[32,136,128]{2,1,0:T(8,128)(2,1)} custom-call(s32[3]{0:T(128)} %dynamic_slice.3.low_ref, s32[2]{0:T(128)} %pad_add_fusion.place_ref, f32[2,2,16,768]{3,2,1,0:T(8,128)} %copy-done, f32[2,2,16,768]{3,2,1,0:T(8,128)} %copy-done.4, bf16[3,768,256]{2,1,0:T(8,128)(2,1)} %columns.2, bf16[4,3,48,768]{3,2,1,0:T(8,128)(2,1)} %pad.13.t0, ...), custom_call_target="tpu_custom_call" | custom-call | flops 1811939328 | bytes 12000000 | tf_op jit(solution)/shard_map/spectral/pallas_call | solution.py:274
  109.8 16.0 %all-to-all-done.4.x_ref = bf16[32,272,128]{2,1,0:T(8,128)(2,1)} async-done(((bf16[32,272,128]{2,1,0:T(8,128)(2,1)}), bf16[32,272,128]{2,1,0:T(8,128)(2,1)}, u32[]{:S(2)}, u32[]{:S(2)}) %all-to-all-start.4) | async-done | bytes 2228256 | tf_op jit(solution)/shard_map/all_to_all | solution.py:381
  125.8 6.3 %all-to-all-start.2 = ((bf16[32,136,128]{2,1,0:T(8,128)(2,1)}), bf16[32,136,128]{2,1,0:T(8,128)(2,1)}, u32[]{:S(2)}, u32[]{:S(2)}) async-start(bf16[32,136,128]{2,1,0:T(8,128)(2,1)} %spectral.2), calls=%async_computation.2 | async-start | bytes 2228224 | tf_op jit(solution)/shard_map/all_to_all | solution.py:382
  132.2 0.8 broadcast_in_dim.2.scale_ref
  133.0 11.4 %inverse.2.done_ref = bf16[3,90,16,1440]{3,2,1,0:T(8,128)(2,1)} custom-call(f32[90,1,512]{2,1,0:T(1,128)} %broadcast_in_dim.2.scale_ref, bf16[1440,512]{1,0:T(8,128)(2,1)} %get-tuple-element.12.table_ref, bf16[32,272,128]{2,1,0:T(8,128)(2,1)} %all-to-all-done.4.x_ref), custom_call_target="tpu_custom_call" | custom-call | flops 8493465600 | bytes 12000000 | tf_op jit(solution)/shard_map/inverse/pallas_call | solution.py:338
  144.4 5.6 %all-to-all-done.2.x_ref = bf16[32,136,128]{2,1,0:T(8,128)(2,1)} async-done(((bf16[32,136,128]{2,1,0:T(8,128)(2,1)}), bf16[32,136,128]{2,1,0:T(8,128)(2,1)}, u32[]{:S(2)}, u32[]{:S(2)}) %all-to-all-start.2) | async-done | bytes 1114144 | tf_op jit(solution)/shard_map/all_to_all | solution.py:382
  150.0 6.8 %inverse.3 = bf16[3,90,16,1440]{3,2,1,0:T(8,128)(2,1)} custom-call(f32[90,1,512]{2,1,0:T(1,128)} %broadcast_in_dim.2.scale_ref, bf16[1440,512]{1,0:T(8,128)(2,1)} %get-tuple-element.12.table_ref, bf16[32,136,128]{2,1,0:T(8,128)(2,1)} %all-to-all-done.2.x_ref, bf16[3,90,16,1440]{3,2,1,0:T(8,128)(2,1)} %inverse.2.done_ref), custom_call_target="tpu_custom_call", output_to_operand_aliasing={{}: (3, {})} | custom-call | flops 4246732800 | bytes 6000000 | tf_op jit(solution)/shard_map/inverse/pallas_call | solution.py:338
  (24 shorter events, 1.6 us)
Async XLA Ops:
  0.0 23.1 %all-to-all-start = ((bf16[4,3,45,768]{3,2,1,0:T(8,128)(2,1)}), bf16[4,3,45,768]{3,2,1,0:T(8,128)(2,1)S(1)}, u32[]{:S(2)}, u32[]{:S(2)}) async-start(bf16[4,3,45,768]{3,2,1,0:T(8,128)(2,1)} %bitcast.14), calls=%async_computation | async-start | bytes 1769472 | tf_op jit(solution)/shard_map/all_to_all | solution.py:364
  6.6 16.4 %collective-permute-start = (f32[2,16,768]{2,1,0:T(8,128)S(1)}, f32[2,16,768]{2,1,0:T(8,128)}, u32[]{:S(2)}, u32[]{:S(2)}) collective-permute-start(f32[2,16,768]{2,1,0:T(8,128)S(1)} %fusion.3), channel_id=1, source_target_pairs={{0,8},{8,0},{1,9},{9,1},{2,10},{10,2},{3,11},{11,3},{4,12},{12,4},... | collective-permute-start | bytes 294920 | tf_op jit(solution)/shard_map/ppermute | solution.py:366
  23.1 35.6 %all-to-all-start.3 = ((bf16[32,272,128]{2,1,0:T(8,128)(2,1)}), bf16[32,272,128]{2,1,0:T(8,128)(2,1)}, u32[]{:S(2)}, u32[]{:S(2)}) async-start(bf16[32,272,128]{2,1,0:T(8,128)(2,1)} %get-tuple-element.18), calls=%async_computation.3 | async-start | bytes 4456448 | tf_op jit(solution)/shard_map/all_to_all | solution.py:371
  29.6 43.1 %collective-permute-start.4 = (bf16[4,3,48,768]{3,2,1,0:T(8,128)(2,1)}, bf16[4,3,48,768]{3,2,1,0:T(8,128)(2,1)}, u32[]{:S(2)}, u32[]{:S(2)}) collective-permute-start(bf16[4,3,48,768]{3,2,1,0:T(8,128)(2,1)} %pad.13.t0), channel_id=1, source_target_pairs={{0,6},{2,0},{4,2},{6,4},{1,7},{3,1},{5,3},{7,5},{8,14},{10,8},{12,... | collective-permute-start | bytes 2654216 | tf_op jit(solution)/shard_map/ppermute | solution.py:373
  33.3 39.4 %collective-permute-start.3 = (bf16[4,3,48,768]{3,2,1,0:T(8,128)(2,1)}, bf16[4,3,48,768]{3,2,1,0:T(8,128)(2,1)}, u32[]{:S(2)}, u32[]{:S(2)}) collective-permute-start(bf16[4,3,48,768]{3,2,1,0:T(8,128)(2,1)} %pad.13.t0), channel_id=1, source_target_pairs={{0,4},{2,6},{4,0},{6,2},{1,5},{3,7},{5,1},{7,3},{8,12},{10,14},{12... | collective-permute-start | bytes 2654216 | tf_op jit(solution)/shard_map/ppermute | solution.py:373
  33.3 41.8 %collective-permute-start.2 = (bf16[4,3,48,768]{3,2,1,0:T(8,128)(2,1)}, bf16[4,3,48,768]{3,2,1,0:T(8,128)(2,1)}, u32[]{:S(2)}, u32[]{:S(2)}) collective-permute-start(bf16[4,3,48,768]{3,2,1,0:T(8,128)(2,1)} %pad.13.t0), channel_id=1, source_target_pairs={{0,2},{2,4},{4,6},{6,0},{1,3},{3,5},{5,7},{7,1},{8,10},{10,12},{12... | collective-permute-start | bytes 2654216 | tf_op jit(solution)/shard_map/ppermute | solution.py:373
  41.2 23.8 %copy-start.1 = (f32[16,720]{1,0:T(8,128)S(1)}, f32[16,720]{1,0:T(8,128)}, u32[]{:S(2)}) copy-start(f32[16,720]{1,0:T(8,128)} %param.9) | copy-start | bytes 138244
  41.2 23.8 %copy-start.2 = (f32[16,720]{1,0:T(8,128)S(1)}, f32[16,720]{1,0:T(8,128)}, u32[]{:S(2)}) copy-start(f32[16,720]{1,0:T(8,128)} %param.8) | copy-start | bytes 138244
  41.2 25.2 %copy-start.3 = (s32[96]{0:T(128)S(1)}, s32[96]{0:T(128)}, u32[]{:S(2)}) copy-start(s32[96]{0:T(128)} %order_ref.3) | copy-start | bytes 1156
  58.7 29.1 %all-to-all-start.1 = ((bf16[32,136,128]{2,1,0:T(8,128)(2,1)}), bf16[32,136,128]{2,1,0:T(8,128)(2,1)}, u32[]{:S(2)}, u32[]{:S(2)}) async-start(bf16[32,136,128]{2,1,0:T(8,128)(2,1)} %forward.3), calls=%async_computation.1 | async-start | bytes 2228224 | tf_op jit(solution)/shard_map/all_to_all | solution.py:375
  65.9 6.8 %copy-start = (f32[2,2,16,768]{3,2,1,0:T(8,128)}, f32[2,2,16,768]{3,2,1,0:T(8,128)S(1)}, u32[]{:S(2)}) copy-start(f32[2,2,16,768]{3,2,1,0:T(8,128)S(1)} %pad_maximum_fusion.f0) | copy-start | bytes 589828
  66.0 6.8 %collective-permute-start.1 = (f32[2,2,16,768]{3,2,1,0:T(8,128)S(1)}, f32[2,2,16,768]{3,2,1,0:T(8,128)S(1)}, u32[]{:S(2)}, u32[]{:S(2)}) collective-permute-start(f32[2,2,16,768]{3,2,1,0:T(8,128)S(1)} %pad_maximum_fusion.f0), channel_id=1, source_target_pairs={{0,1},{1,0},{2,3},{3,2},{4,5},{5,4},{6,7},{7,6},{8,9},{9,8},{10,11... | collective-permute-start | bytes 589832 | tf_op jit(solution)/shard_map/ppermute | solution.py:377
  72.7 2.4 %copy-start.4 = (f32[2,2,16,768]{3,2,1,0:T(8,128)}, f32[2,2,16,768]{3,2,1,0:T(8,128)S(1)}, u32[]{:S(2)}) copy-start(f32[2,2,16,768]{3,2,1,0:T(8,128)S(1)} %collective-permute-done.1.f1) | copy-start | bytes 589828
  87.8 38.0 %all-to-all-start.4 = ((bf16[32,272,128]{2,1,0:T(8,128)(2,1)}), bf16[32,272,128]{2,1,0:T(8,128)(2,1)}, u32[]{:S(2)}, u32[]{:S(2)}) async-start(bf16[32,272,128]{2,1,0:T(8,128)(2,1)} %spectral.3), calls=%async_computation.4 | async-start | bytes 4456448 | tf_op jit(solution)/shard_map/all_to_all | solution.py:381
  109.8 22.3 %copy-start.5 = (f32[90]{0:T(128)S(1)}, f32[90]{0:T(128)}, u32[]{:S(2)}) copy-start(f32[90]{0:T(128)} %param.10) | copy-start | bytes 1084
  125.8 24.2 %all-to-all-start.2 = ((bf16[32,136,128]{2,1,0:T(8,128)(2,1)}), bf16[32,136,128]{2,1,0:T(8,128)(2,1)}, u32[]{:S(2)}, u32[]{:S(2)}) async-start(bf16[32,136,128]{2,1,0:T(8,128)(2,1)} %spectral.2), calls=%async_computation.2 | async-start | bytes 2228224 | tf_op jit(solution)/shard_map/all_to_all | solution.py:382

commit v5 on v4

--- a/solution.py
+++ b/solution.py
@@ -14,7 +14,7 @@
 ROWS = 768
 PAIRS = 96
 SAMPLES = 3
-EARLY = 2
+EARLY = 1
 EXTRA = 8
 CH = 16
 LAT = 90

time: 158 us -> 181 us (1.15)
  waiting for transfers between devices: 41.5 us -> 65 us
    ppermute x3, waiting for transfers between devices: 2.36 us -> 33.5 us  [body(): lax.ppermute(own, 'z', [(i, (i + shift) % 4) for i in range(4)])]
    all_to_all x1, waiting for transfers between devices: 5.61 us -> 22.5 us  [body(): lax.all_to_all(spectral(low, where, filters, late, tables, SAMPLES - EARL...]
    all_to_all x1, waiting for transfers between devices: 16 us -> 0.01 us  [body(): lax.all_to_all(spectral(low, where, filters, early, tables, EARLY), SLOT_...]
    all_to_all x1, waiting for transfers between devices: 17.5 us -> 5.71 us  [body(): early = lax.all_to_all(packed, SLOT_AXES, 0, 0)]
    ppermute x1, waiting for transfers between devices: 0.01 us -> 3.25 us  [body(): lax.ppermute(padded_filters(filter_re, filter_im), 'x_hi', [(0, 1), (1, 0)])]
  transfers between devices with their start and end apart: 10 -> 10, of which waited for: 4 -> 5; matrix products, arithmetic and copies ran while one was open for 3% -> 3% of each run, Pallas kernels for 41% -> 33%
where the time goes in v5:
time: 181 us
  Pallas kernels  71 us (39%)
  waiting for transfers between devices  65 us (36%)
  starting transfers between devices  39.6 us (22%)
  local copies, waits for them, and re-layouts  2.49 us (1%)
  other arithmetic  2.35 us (1%)
    ppermute x3, waiting for transfers between devices, body(): lax.ppermute(own, 'z', [(i, (i + shift) % 4) for i in range(4)])  33.5 us
    pallas_call x2, Pallas kernels, spectral(): pl.pallas_call(functools.partial(spectral_kernel, count), grid=(SLOTS,),...  22.6 us
    all_to_all x1, waiting for transfers between devices, body(): lax.all_to_all(spectral(low, where, filters, late, tables, SAMPLES - EARL...  22.5 us
    pallas_call x2, Pallas kernels, forward(): pl.pallas_call(first_forward_kernel if table is None else later_forward_k...  20.6 us
    pallas_call x2, Pallas kernels, inverse(): pl.pallas_call(inverse_kernel if done is None else later_inverse_kernel,...  18.2 us
    pallas_call x2, Pallas kernels, columns_of(): pl.pallas_call(functools.partial(columns_kernel, count), grid=(SLOTS,), i...  9.52 us
    all_to_all x1, starting transfers between devices, body(): lax.all_to_all(spectral(low, where, filters, early, tables, EARLY), SLOT_...  7.64 us
    all_to_all x1, starting transfers between devices, body(): lax.all_to_all(spectral(low, where, filters, late, tables, SAMPLES - EARL...  7.44 us
  transfers between devices with their start and end apart: 10, of which 5 were waited for; matrix products, arithmetic and copies ran while one was open for 3% of the time, Pallas kernels for 33%

profile of v5, /device:TPU:1, one launch (start us, length us, event | category | flops | bytes accessed | tf_op | source)
XLA Modules:
  0.0 180.5 jit_solution(6691942683755489629)
XLA Ops:
  0.0 5.8 %all-to-all-start = ((bf16[4,3,45,768]{3,2,1,0:T(8,128)(2,1)}), bf16[4,3,45,768]{3,2,1,0:T(8,128)(2,1)S(1)}, u32[]{:S(2)}, u32[]{:S(2)}) async-start(bf16[4,3,45,768]{3,2,1,0:T(8,128)(2,1)} %bitcast.12), calls=%async_computation | async-start | bytes 1769472 | tf_op jit(solution)/shard_map/all_to_all | solution.py:364
  5.8 0.8 fusion.3
  6.6 3.0 %collective-permute-start = (f32[2,16,768]{2,1,0:T(8,128)S(1)}, f32[2,16,768]{2,1,0:T(8,128)}, u32[]{:S(2)}, u32[]{:S(2)}) collective-permute-start(f32[2,16,768]{2,1,0:T(8,128)S(1)} %fusion.3), channel_id=1, source_target_pairs={{0,8},{8,0},{1,9},{9,1},{2,10},{10,2},{3,11},{11,3},{4,12},{12,4},... | collective-permute-start | bytes 294920 | tf_op jit(solution)/shard_map/ppermute | solution.py:366
  9.6 8.5 %forward.2 = (bf16[32,136,128]{2,1,0:T(8,128)(2,1)}, bf16[1440,512]{1,0:T(8,128)(2,1)}) custom-call(s32[96]{0:T(128)} %order_ref.3, bf16[3,90,16,1440]{3,2,1,0:T(8,128)(2,1)} %bitcast.17), custom_call_target="tpu_custom_call" | custom-call | flops 4246732800 | bytes 6000000 | tf_op jit(solution)/shard_map/forward/pallas_call | solution.py:143
  18.1 3.3 %collective-permute-done = f32[2,16,768]{2,1,0:T(8,128)} collective-permute-done((f32[2,16,768]{2,1,0:T(8,128)S(1)}, f32[2,16,768]{2,1,0:T(8,128)}, u32[]{:S(2)}, u32[]{:S(2)}) %collective-permute-start) | collective-permute-done | bytes 98336 | tf_op jit(solution)/shard_map/ppermute | solution.py:366
  21.4 5.7 %all-to-all-start.3 = ((bf16[32,136,128]{2,1,0:T(8,128)(2,1)}), bf16[32,136,128]{2,1,0:T(8,128)(2,1)}, u32[]{:S(2)}, u32[]{:S(2)}) async-start(bf16[32,136,128]{2,1,0:T(8,128)(2,1)} %get-tuple-element.18), calls=%async_computation.3 | async-start | bytes 2228224 | tf_op jit(solution)/shard_map/all_to_all | solution.py:371
  27.0 12.1 %forward.3 = bf16[32,272,128]{2,1,0:T(8,128)(2,1)} custom-call(s32[96]{0:T(128)} %order_ref.3, bf16[3,90,16,1440]{3,2,1,0:T(8,128)(2,1)} %bitcast.18, bf16[1440,512]{1,0:T(8,128)(2,1)} %get-tuple-element.12.table_ref), custom_call_target="tpu_custom_call" | custom-call | flops 8493465600 | bytes 12000000 | tf_op jit(solution)/shard_map/forward/pallas_call | solution.py:143
  39.1 5.7 %all-to-all-done.3.x_ref = bf16[32,136,128]{2,1,0:T(8,128)(2,1)} async-done(((bf16[32,136,128]{2,1,0:T(8,128)(2,1)}), bf16[32,136,128]{2,1,0:T(8,128)(2,1)}, u32[]{:S(2)}, u32[]{:S(2)}) %all-to-all-start.3) | async-done | bytes 1114144 | tf_op jit(solution)/shard_map/all_to_all | solution.py:371
  44.8 4.6 %all-to-all-start.1 = ((bf16[32,272,128]{2,1,0:T(8,128)(2,1)}), bf16[32,272,128]{2,1,0:T(8,128)(2,1)}, u32[]{:S(2)}, u32[]{:S(2)}) async-start(bf16[32,272,128]{2,1,0:T(8,128)(2,1)} %forward.3), calls=%async_computation.1 | async-start | bytes 4456448 | tf_op jit(solution)/shard_map/all_to_all | solution.py:375
  49.5 1.0 pad.13.t0
  50.4 3.8 %collective-permute-start.4 = (bf16[4,3,48,768]{3,2,1,0:T(8,128)(2,1)}, bf16[4,3,48,768]{3,2,1,0:T(8,128)(2,1)}, u32[]{:S(2)}, u32[]{:S(2)}) collective-permute-start(bf16[4,3,48,768]{3,2,1,0:T(8,128)(2,1)} %pad.13.t0), channel_id=1, source_target_pairs={{0,6},{2,0},{4,2},{6,4},{1,7},{3,1},{5,3},{7,5},{8,14},{10,8},{12,... | collective-permute-start | bytes 2654216 | tf_op jit(solution)/shard_map/ppermute | solution.py:373
  54.9 0.9 pad_maximum_fusion.f0
  55.8 1.1 collective-permute-start.1
  58.2 4.3 %columns.3 = bf16[3,768,256]{2,1,0:T(8,128)(2,1)} custom-call(bf16[32,136,128]{2,1,0:T(8,128)(2,1)} %all-to-all-done.3.x_ref), custom_call_target="tpu_custom_call" | custom-call | flops 10000000 | bytes 5000000 | tf_op jit(solution)/shard_map/columns/pallas_call | solution.py:195
  62.5 29.9 %collective-permute-done.4.t3 = bf16[4,3,48,768]{3,2,1,0:T(8,128)(2,1)} collective-permute-done((bf16[4,3,48,768]{3,2,1,0:T(8,128)(2,1)}, bf16[4,3,48,768]{3,2,1,0:T(8,128)(2,1)}, u32[]{:S(2)}, u32[]{:S(2)}) %collective-permute-start.4) | collective-permute-done | bytes 884768 | tf_op jit(solution)/shard_map/ppermute | solution.py:373
  92.4 3.6 %collective-permute-done.2.t1 = bf16[4,3,48,768]{3,2,1,0:T(8,128)(2,1)} collective-permute-done((bf16[4,3,48,768]{3,2,1,0:T(8,128)(2,1)}, bf16[4,3,48,768]{3,2,1,0:T(8,128)(2,1)}, u32[]{:S(2)}, u32[]{:S(2)}) %collective-permute-start.2) | collective-permute-done | bytes 884768 | tf_op jit(solution)/shard_map/ppermute | solution.py:373
  96.0 9.9 %spectral.3 = bf16[32,136,128]{2,1,0:T(8,128)(2,1)} custom-call(s32[3]{0:T(128)} %dynamic_slice.3.low_ref, s32[2]{0:T(128)} %pad_add_fusion.place_ref, f32[2,2,16,768]{3,2,1,0:T(8,128)} %copy-done, f32[2,2,16,768]{3,2,1,0:T(8,128)} %copy-done.3, bf16[3,768,256]{2,1,0:T(8,128)(2,1)} %columns.3, bf16[4,3,48,768]{3,2,1,0:T(8,128)(2,1)} %pad.13.t0, ...), custom_call_target="tpu_custom_call" | custom-call | flops 1811939328 | bytes 12000000 | tf_op jit(solution)/shard_map/spectral/pallas_call | solution.py:274
  105.9 7.6 %all-to-all-start.4 = ((bf16[32,136,128]{2,1,0:T(8,128)(2,1)}), bf16[32,136,128]{2,1,0:T(8,128)(2,1)}, u32[]{:S(2)}, u32[]{:S(2)}) async-start(bf16[32,136,128]{2,1,0:T(8,128)(2,1)} %spectral.3), calls=%async_computation.4 | async-start | bytes 2228224 | tf_op jit(solution)/shard_map/all_to_all | solution.py:381
  113.6 5.2 %columns.2 = bf16[3,768,512]{2,1,0:T(8,128)(2,1)} custom-call(bf16[32,272,128]{2,1,0:T(8,128)(2,1)} %all-to-all-done.1.x_ref), custom_call_target="tpu_custom_call" | custom-call | flops 10000000 | bytes 5000000 | tf_op jit(solution)/shard_map/columns/pallas_call | solution.py:195
  118.8 12.7 %spectral.2 = bf16[32,272,128]{2,1,0:T(8,128)(2,1)} custom-call(s32[3]{0:T(128)} %dynamic_slice.3.low_ref, s32[2]{0:T(128)} %pad_add_fusion.place_ref, f32[2,2,16,768]{3,2,1,0:T(8,128)} %copy-done, f32[2,2,16,768]{3,2,1,0:T(8,128)} %copy-done.3, bf16[3,768,512]{2,1,0:T(8,128)(2,1)} %columns.2, bf16[4,3,48,768]{3,2,1,0:T(8,128)(2,1)} %pad.13.t0, ...), custom_call_target="tpu_custom_call" | custom-call | flops 3623878656 | bytes 12000000 | tf_op jit(solution)/shard_map/spectral/pallas_call | solution.py:274
  131.6 7.4 %all-to-all-start.2 = ((bf16[32,272,128]{2,1,0:T(8,128)(2,1)}), bf16[32,272,128]{2,1,0:T(8,128)(2,1)}, u32[]{:S(2)}, u32[]{:S(2)}) async-start(bf16[32,272,128]{2,1,0:T(8,128)(2,1)} %spectral.2), calls=%async_computation.2 | async-start | bytes 4456448 | tf_op jit(solution)/shard_map/all_to_all | solution.py:382
  139.9 6.8 %inverse.2.done_ref = bf16[3,90,16,1440]{3,2,1,0:T(8,128)(2,1)} custom-call(f32[90,1,512]{2,1,0:T(1,128)} %broadcast_in_dim.2.scale_ref, bf16[1440,512]{1,0:T(8,128)(2,1)} %get-tuple-element.12.table_ref, bf16[32,136,128]{2,1,0:T(8,128)(2,1)} %all-to-all-done.4.x_ref), custom_call_target="tpu_custom_call" | custom-call | flops 4246732800 | bytes 6000000 | tf_op jit(solution)/shard_map/inverse/pallas_call | solution.py:338
  146.7 22.5 %all-to-all-done.2.x_ref = bf16[32,272,128]{2,1,0:T(8,128)(2,1)} async-done(((bf16[32,272,128]{2,1,0:T(8,128)(2,1)}), bf16[32,272,128]{2,1,0:T(8,128)(2,1)}, u32[]{:S(2)}, u32[]{:S(2)}) %all-to-all-start.2) | async-done | bytes 2228256 | tf_op jit(solution)/shard_map/all_to_all | solution.py:382
  169.2 11.4 %inverse.3 = bf16[3,90,16,1440]{3,2,1,0:T(8,128)(2,1)} custom-call(f32[90,1,512]{2,1,0:T(1,128)} %broadcast_in_dim.2.scale_ref, bf16[1440,512]{1,0:T(8,128)(2,1)} %get-tuple-element.12.table_ref, bf16[32,272,128]{2,1,0:T(8,128)(2,1)} %all-to-all-done.2.x_ref, bf16[3,90,16,1440]{3,2,1,0:T(8,128)(2,1)} %inverse.2.done_ref), custom_call_target="tpu_custom_call", output_to_operand_aliasing={{}: (3, {})} | custom-call | flops 8493465600 | bytes 12000000 | tf_op jit(solution)/shard_map/inverse/pallas_call | solution.py:338
  (24 shorter events, 2.8 us)
Async XLA Ops:
  0.0 21.4 %all-to-all-start = ((bf16[4,3,45,768]{3,2,1,0:T(8,128)(2,1)}), bf16[4,3,45,768]{3,2,1,0:T(8,128)(2,1)S(1)}, u32[]{:S(2)}, u32[]{:S(2)}) async-start(bf16[4,3,45,768]{3,2,1,0:T(8,128)(2,1)} %bitcast.12), calls=%async_computation | async-start | bytes 1769472 | tf_op jit(solution)/shard_map/all_to_all | solution.py:364
  6.6 14.7 %collective-permute-start = (f32[2,16,768]{2,1,0:T(8,128)S(1)}, f32[2,16,768]{2,1,0:T(8,128)}, u32[]{:S(2)}, u32[]{:S(2)}) collective-permute-start(f32[2,16,768]{2,1,0:T(8,128)S(1)} %fusion.3), channel_id=1, source_target_pairs={{0,8},{8,0},{1,9},{9,1},{2,10},{10,2},{3,11},{11,3},{4,12},{12,4},... | collective-permute-start | bytes 294920 | tf_op jit(solution)/shard_map/ppermute | solution.py:366
  21.4 23.5 %all-to-all-start.3 = ((bf16[32,136,128]{2,1,0:T(8,128)(2,1)}), bf16[32,136,128]{2,1,0:T(8,128)(2,1)}, u32[]{:S(2)}, u32[]{:S(2)}) async-start(bf16[32,136,128]{2,1,0:T(8,128)(2,1)} %get-tuple-element.18), calls=%async_computation.3 | async-start | bytes 2228224 | tf_op jit(solution)/shard_map/all_to_all | solution.py:371
  39.1 15.8 %copy-start.1 = (f32[16,720]{1,0:T(8,128)S(1)}, f32[16,720]{1,0:T(8,128)}, u32[]{:S(2)}) copy-start(f32[16,720]{1,0:T(8,128)} %param.9) | copy-start | bytes 138244
  39.1 15.8 %copy-start.2 = (f32[16,720]{1,0:T(8,128)S(1)}, f32[16,720]{1,0:T(8,128)}, u32[]{:S(2)}) copy-start(f32[16,720]{1,0:T(8,128)} %param.8) | copy-start | bytes 138244
  44.8 61.1 %all-to-all-start.1 = ((bf16[32,272,128]{2,1,0:T(8,128)(2,1)}), bf16[32,272,128]{2,1,0:T(8,128)(2,1)}, u32[]{:S(2)}, u32[]{:S(2)}) async-start(bf16[32,272,128]{2,1,0:T(8,128)(2,1)} %forward.3), calls=%async_computation.1 | async-start | bytes 4456448 | tf_op jit(solution)/shard_map/all_to_all | solution.py:375
  49.5 7.5 %copy-start.4 = (s32[96]{0:T(128)S(1)}, s32[96]{0:T(128)}, u32[]{:S(2)}) copy-start(s32[96]{0:T(128)} %order_ref.3) | copy-start | bytes 1156
  50.4 41.9 %collective-permute-start.4 = (bf16[4,3,48,768]{3,2,1,0:T(8,128)(2,1)}, bf16[4,3,48,768]{3,2,1,0:T(8,128)(2,1)}, u32[]{:S(2)}, u32[]{:S(2)}) collective-permute-start(bf16[4,3,48,768]{3,2,1,0:T(8,128)(2,1)} %pad.13.t0), channel_id=1, source_target_pairs={{0,6},{2,0},{4,2},{6,4},{1,7},{3,1},{5,3},{7,5},{8,14},{10,8},{12,... | collective-permute-start | bytes 2654216 | tf_op jit(solution)/shard_map/ppermute | solution.py:373
  54.2 38.2 %collective-permute-start.3 = (bf16[4,3,48,768]{3,2,1,0:T(8,128)(2,1)}, bf16[4,3,48,768]{3,2,1,0:T(8,128)(2,1)}, u32[]{:S(2)}, u32[]{:S(2)}) collective-permute-start(bf16[4,3,48,768]{3,2,1,0:T(8,128)(2,1)} %pad.13.t0), channel_id=1, source_target_pairs={{0,4},{2,6},{4,0},{6,2},{1,5},{3,7},{5,1},{7,3},{8,12},{10,14},{12... | collective-permute-start | bytes 2654216 | tf_op jit(solution)/shard_map/ppermute | solution.py:373
  54.2 41.8 %collective-permute-start.2 = (bf16[4,3,48,768]{3,2,1,0:T(8,128)(2,1)}, bf16[4,3,48,768]{3,2,1,0:T(8,128)(2,1)}, u32[]{:S(2)}, u32[]{:S(2)}) collective-permute-start(bf16[4,3,48,768]{3,2,1,0:T(8,128)(2,1)} %pad.13.t0), channel_id=1, source_target_pairs={{0,2},{2,4},{4,6},{6,0},{1,3},{3,5},{5,7},{7,1},{8,10},{10,12},{12... | collective-permute-start | bytes 2654216 | tf_op jit(solution)/shard_map/ppermute | solution.py:373
  55.8 40.2 %copy-start = (f32[2,2,16,768]{3,2,1,0:T(8,128)}, f32[2,2,16,768]{3,2,1,0:T(8,128)S(1)}, u32[]{:S(2)}) copy-start(f32[2,2,16,768]{3,2,1,0:T(8,128)S(1)} %pad_maximum_fusion.f0) | copy-start | bytes 589828
  55.8 6.6 %collective-permute-start.1 = (f32[2,2,16,768]{3,2,1,0:T(8,128)S(1)}, f32[2,2,16,768]{3,2,1,0:T(8,128)S(1)}, u32[]{:S(2)}, u32[]{:S(2)}) collective-permute-start(f32[2,2,16,768]{3,2,1,0:T(8,128)S(1)} %pad_maximum_fusion.f0), channel_id=1, source_target_pairs={{0,1},{1,0},{2,3},{3,2},{4,5},{5,4},{6,7},{7,6},{8,9},{9,8},{10,11... | collective-permute-start | bytes 589832 | tf_op jit(solution)/shard_map/ppermute | solution.py:377
  62.5 33.5 %copy-start.3 = (f32[2,2,16,768]{3,2,1,0:T(8,128)}, f32[2,2,16,768]{3,2,1,0:T(8,128)S(1)}, u32[]{:S(2)}) copy-start(f32[2,2,16,768]{3,2,1,0:T(8,128)S(1)} %collective-permute-done.1.f1) | copy-start | bytes 589828
  105.9 25.6 %all-to-all-start.4 = ((bf16[32,136,128]{2,1,0:T(8,128)(2,1)}), bf16[32,136,128]{2,1,0:T(8,128)(2,1)}, u32[]{:S(2)}, u32[]{:S(2)}) async-start(bf16[32,136,128]{2,1,0:T(8,128)(2,1)} %spectral.3), calls=%async_computation.4 | async-start | bytes 2228224 | tf_op jit(solution)/shard_map/all_to_all | solution.py:381
  131.5 7.5 %copy-start.5 = (f32[90]{0:T(128)S(1)}, f32[90]{0:T(128)}, u32[]{:S(2)}) copy-start(f32[90]{0:T(128)} %param.10) | copy-start | bytes 1084
  131.6 37.6 %all-to-all-start.2 = ((bf16[32,272,128]{2,1,0:T(8,128)(2,1)}), bf16[32,272,128]{2,1,0:T(8,128)(2,1)}, u32[]{:S(2)}, u32[]{:S(2)}) async-start(bf16[32,272,128]{2,1,0:T(8,128)(2,1)} %spectral.2), calls=%async_computation.2 | async-start | bytes 4456448 | tf_op jit(solution)/shard_map/all_to_all | solution.py:382
